TPU v7x, 512 devices: a whole 4x4x16 slice. The times are simulated.
512 devices in a mesh: dp: 128 (over z, y, core), tensor: 4 (over x).
Axes of the slice: x: 4, y: 4, z: 16, core: 2. Of those that a mesh axis runs over, the one named last changes fastest.
Arguments:
- patches: bfloat16 [131072, 1280], P('dp', 'tensor'), may hold values from -60 to 60
- counts: int32 [256], replicated, may hold values from 0 to 512, as said below
- first_gain: float32 [1280], replicated, may hold values from 0.1 to 1.9
- first_shift: float32 [1280], replicated, may hold values from -3 to 3
- in_weight: bfloat16 [1280, 3, 1280], P(None, None, 'tensor'), may hold values from -0.15625 to 0.15625
- in_bias: float32 [3, 1280], P(None, 'tensor'), may hold values from -30 to 30
- out_weight: bfloat16 [1280, 1280], P(None, 'tensor'), may hold values from -0.15625 to 0.15625
- out_bias: float32 [1280], P('tensor'), may hold values from -3 to 3
- second_gain: float32 [1280], P('tensor'), may hold values from 0.1 to 1.9
- second_shift: float32 [1280], P('tensor'), may hold values from -3 to 3
- merger_weight: bfloat16 [4, 1280, 4096], P(None, 'tensor', 'dp'), may hold values from -0.078125 to 0.078125
- merger_bias: float32 [4096], replicated, may hold values from -4 to 4
Outputs:
- embeds: bfloat16 [32768, 4096], P(('dp', 'tensor'))
Inputs may be any that keep to these rules, and one draw needn't show every extreme that they name: Entry 2 r + j is the patch count of slot j of data rank r, 0 for an empty slot; a rank's images fill its slots from slot 0; counts are multiples of 4; ranks 2 i and 2 i + 1 hold at most two images together, and in every draw some rank holds two.
All inputs are finite; a program needn't handle non-finite values.
Results may differ from a plain program's by a relative error of at most 0.0095.
Values may be sent and summed in bfloat16 or wider, within the bound.
A program may use at most 128 MiB of HBM per device.

v0:
```python
import math

import jax
import jax.numpy as jnp
from jax import lax
from jax.sharding import PartitionSpec as P

D = 1280
HEADS = 16
TILE = 512
SLOTS = 2


EPS = 1e-06
MASKED = -1e30


def sent_to_all(x, axis):
    copies = jnp.broadcast_to(x, (lax.axis_size(axis), *x.shape))
    return lax.all_to_all(copies, axis, split_axis=0, concat_axis=0, tiled=True)


def laid_out(pieces, dim):
    pieces = jnp.moveaxis(pieces, 0, dim)
    dims = pieces.shape
    return pieces.reshape(*dims[:dim], dims[dim] * dims[dim + 1], *dims[dim + 2 :])


def collect(x, axis, dim):
    pieces = sent_to_all(x, axis)
    return laid_out(pieces, dim)


def of_everyone(x, axis):
    everything = sent_to_all(x, axis)
    return jnp.sum(everything, axis=0)


def in_one(arrays, axis):
    ends = [0]
    for a in arrays:
        ends.append(ends[-1] + a.size)
    so_far = of_everyone(jnp.concatenate([a.ravel() for a in arrays]), axis)
    return tuple((so_far[b:e].reshape(a.shape) for a, b, e in zip(arrays, ends, ends[1:])))


def in_blocks(x, dim, size):
    before, after = (x.shape[:dim], x.shape[dim + 1 :])
    return jnp.moveaxis(x.reshape(*before, size, -1, *after), dim, 0)


def summed_on_arrival(x, axis, dim):
    pieces = in_blocks(x, dim, lax.axis_size(axis))
    arrived = lax.all_to_all(pieces, axis, split_axis=0, concat_axis=0, tiled=True)
    return arrived.astype(jnp.float32).sum(axis=0)


def layer_norm(values, gain, shift):
    row_mean = jnp.mean(values, axis=-1, keepdims=True)
    centred = values - row_mean
    spread = jnp.mean(centred * centred, axis=-1, keepdims=True)
    return centred * lax.rsqrt(spread + EPS) * gain + shift


def encode(
    shard,
    slot_counts,
    first_gain,
    first_shift,
    in_weight,
    in_bias,
    out_weight,
    out_bias,
    second_gain,
    second_shift,
):
    number = slot_counts.shape[0]
    local_width = shard.shape[1]
    head_size = D // HEADS
    local_heads = local_width // head_size
    scale = 1.0 / math.sqrt(head_size)
    whole = collect(shard, "tensor", 1)
    values = whole.astype(jnp.float32)
    normed = layer_norm(values, first_gain, first_shift).astype(jnp.bfloat16)
    projected = jnp.dot(
        normed, in_weight.reshape(D, 3 * local_width), preferred_element_type=jnp.float32
    )
    projected = (projected + in_bias.reshape(3 * local_width)).astype(jnp.bfloat16)
    projected = projected.reshape(number, TILE, 3, local_heads, head_size)
    queries = projected[:, :, 0]
    keys_tile = projected[:, :, 1]
    values_tile = projected[:, :, 2]
    scores = (
        jnp.einsum("nqhd,nkhd->nhqk", queries, keys_tile, preferred_element_type=jnp.float32)
        * scale
    )
    positions = jnp.arange(TILE, dtype=jnp.int32)
    key_live = positions[None, :] < slot_counts[:, None]
    scores = jnp.where(key_live[:, None, None, :], scores, MASKED)
    highest = jnp.max(scores, axis=-1, keepdims=True)
    raised = jnp.exp(scores - highest)
    weights = (raised / jnp.sum(raised, axis=-1, keepdims=True)).astype(jnp.bfloat16)
    heads_out = jnp.einsum(
        "nhqk,nkhd->nqhd", weights, values_tile, preferred_element_type=jnp.float32
    )
    heads_out = heads_out.astype(jnp.bfloat16).reshape(number * TILE, local_width)
    all_heads = collect(heads_out, "tensor", 1)
    residual = (
        shard.astype(jnp.float32)
        + jnp.dot(all_heads, out_weight, preferred_element_type=jnp.float32)
        + out_bias
    )
    row_sum, row_squares = in_one(
        (jnp.sum(residual, axis=1), jnp.sum(residual * residual, axis=1)), "tensor"
    )
    row_mean = (row_sum / D)[:, None]
    second = (row_squares / D)[:, None]
    encoded = (residual - row_mean) * lax.rsqrt(
        second - row_mean * row_mean + EPS
    ) * second_gain + second_shift
    return encoded.astype(jnp.bfloat16).reshape(number * TILE // 4, 4 * local_width)


def per_device(
    patches,
    counts,
    first_gain,
    first_shift,
    in_weight,
    in_bias,
    out_weight,
    out_bias,
    second_gain,
    second_shift,
    merger_weight,
    merger_bias,
):
    rank = lax.axis_index("dp")
    mine = lax.dynamic_slice_in_dim(counts, rank * SLOTS, SLOTS)
    weights_args = (
        first_gain,
        first_shift,
        in_weight,
        in_bias,
        out_weight,
        out_bias,
        second_gain,
        second_shift,
    )
    merged = encode(patches, mine, *weights_args)
    groups = lax.axis_size("tensor")
    quarter = SLOTS * TILE // 4 // groups
    piece = lax.all_gather(merger_weight, "dp", axis=2, tiled=True)
    partial_value = jnp.dot(
        merged, piece.reshape(-1, piece.shape[2]), preferred_element_type=jnp.float32
    )
    summed = summed_on_arrival(partial_value.astype(jnp.bfloat16), "tensor", 0)
    mixed = (summed + merger_bias).astype(jnp.bfloat16)
    row_index = lax.axis_index("tensor") * quarter + jnp.arange(quarter, dtype=jnp.int32)
    slot_of_row = row_index // (TILE // 4)
    within = row_index % (TILE // 4)
    row_count = jnp.sum(
        jnp.where(
            slot_of_row[:, None] == jnp.arange(SLOTS, dtype=jnp.int32)[None, :], mine[None, :], 0
        ),
        axis=1,
    )
    keep = (within * 4 < row_count)[:, None]
    return jnp.where(keep, mixed, jnp.zeros_like(mixed))


def solution(mesh):
    return jax.shard_map(
        per_device,
        mesh=mesh,
        in_specs=(
            P("dp", "tensor"),
            P(),
            P(),
            P(),
            P(None, None, "tensor"),
            P(None, "tensor"),
            P(None, "tensor"),
            P("tensor"),
            P("tensor"),
            P("tensor"),
            P(None, "tensor", "dp"),
            P(),
        ),
        out_specs=P(("dp", "tensor"), None),
        check_vma=False,
    )
```

profile of v0, /device:TPU:1, one launch (start us, length us, event | category | flops | bytes accessed | tf_op | source)
XLA Modules:
  0.0 236.7 jit_solution(9412627003668541712)
XLA Ops:
  6.5 0.0 copy-start
  6.5 0.0 all-gather.2.cloned.1.call-start
  6.5 1.7 copy.48
  8.3 0.0 all-gather.2.cloned.1.call-update
  8.3 2.9 %broadcast_in_dim.40 = bf16[4,1024,320]{1,2,0:T(8,128)(2,1)} broadcast(bf16[1024,320]{0,1:T(8,128)(2,1)} %param.12), dimensions={1,2} | broadcast | bytes 3276800 | tf_op jit(solution)/shard_map/broadcast_in_dim | solution.py:19
  11.2 0.0 copy-start.6
  11.2 0.0 copy-start.4
  11.2 0.0 copy-start.5
  11.2 0.0 copy-start.11
  11.2 5.0 %all-to-all-start = ((bf16[4,1024,320]{1,2,0:T(8,128)(2,1)}), bf16[4,1024,320]{1,2,0:T(8,128)(2,1)}, u32[]{:S(2)}, u32[]{:S(2)}) async-start(bf16[4,1024,320]{1,2,0:T(8,128)(2,1)} %broadcast_in_dim.40), calls=%async_computation | async-start | bytes 5242880 | tf_op jit(solution)/shard_map/all_to_all | solution.py:20
  16.2 0.0 copy-done.6
  16.2 0.1 add.99
  16.3 0.0 copy-done.4
  16.3 0.1 mul.81
  16.3 0.0 copy-done.5
  16.3 0.1 add.96
  16.4 0.0 copy-done.11
  16.4 0.1 dynamic_slice.3
  16.5 0.1 iota_compare_fusion
  16.6 25.8 %all-to-all-done = bf16[4,1024,320]{1,2,0:T(8,128)(2,1)} async-done(((bf16[4,1024,320]{1,2,0:T(8,128)(2,1)}), bf16[4,1024,320]{1,2,0:T(8,128)(2,1)}, u32[]{:S(2)}, u32[]{:S(2)}) %all-to-all-start) | async-done | bytes 2621472 | tf_op jit(solution)/shard_map/all_to_all | solution.py:20
  42.4 2.2 convert_reduce_fusion
  44.6 2.5 %fusion.4 = f32[1024]{0:T(1024)S(1)} fusion(bf16[4,1024,320]{1,2,0:T(8,128)(2,1)} %all-to-all-done, f32[1024]{0:T(1024)S(1)} %broadcast_multiply_fusion), kind=kLoop, calls=%fused_computation.9 | loop fusion | flops 5241856 | bytes 2629632 | tf_op jit(solution)/shard_map/reduce_sum | solution.py:61
  47.1 2.4 %fusion.7 = bf16[4,1024,320]{1,2,0:T(8,128)(2,1)S(1)} fusion(bf16[4,1024,320]{1,2,0:T(8,128)(2,1)} %all-to-all-done, f32[4,320]{1,0:T(4,128)S(1)} %add.96, f32[4,320]{1,0:T(4,128)S(1)} %mul.81, f32[1024]{0:T(1024)S(1)} %add_rsqrt_fusion, f32[1024]{0:T(1024)S(1)} %broadcast_multiply_fusion), kind=kLoop, calls=%fused_computation.12 | loop fusion | flops 7864320 | bytes 5261312 | tf_op jit(solution)/shard_map/convert_element_type | solution.py:84
  49.5 0.0 copy-done
  49.5 3.9 %add_convert_fusion = bf16[1024,960]{0,1:T(8,128)(2,1)} fusion(f32[960]{0:T(1024)S(1)} %add.99, bf16[1280,960]{0,1:T(8,128)(2,1)S(1)} %bitcast.49, bf16[1024,1280]{0,1:T(8,128)(2,1)S(1)} %bitcast.53), kind=kOutput, calls=%fused_computation.19 | convolution fusion | flops 2518548480 | bytes 7048960 | tf_op jit(solution)/shard_map/dot_general | solution.py:85
  53.4 5.8 %reshape.134 = bf16[2,512,3,4,80]{1,0,4,3,2:T(2,128)(2,1)} reshape(bf16[1024,960]{0,1:T(8,128)(2,1)} %add_convert_fusion) | data formatting | bytes 3932160 | tf_op jit(solution)/shard_map/reshape | solution.py:89
  59.2 3.4 %fusion.28 = (bf16[2,512,1,4,80]{1,0,4,3,2:T(2,128)(2,1)S(1)}, bf16[2,512,1,4,80]{1,0,4,3,2:T(2,128)(2,1)}, bf16[2,512,1,4,80]{1,0,4,3,2:T(2,128)(2,1)}) fusion(bf16[2,512,3,4,80]{1,0,4,3,2:T(2,128)(2,1)} %reshape.134), kind=kLoop, calls=%fused_computation.55 | loop fusion | bytes 3932160 | tf_op jit(solution)/shard_map/slice | solution.py:92
  62.6 7.9 %fusion.29 = (f32[2,4,512]{2,1,0:T(4,128)S(1)}, f32[2,4,512,512]{2,3,1,0:T(8,128)}) fusion(pred[2,512]{1,0:T(4,128)(4,1)S(1)} %iota_compare_fusion, bf16[2,512,1,4,80]{1,0,4,3,2:T(2,128)(2,1)} %get-tuple-element.8, bf16[2,512,1,4,80]{1,0,4,3,2:T(2,128)(2,1)} %get-tuple-element.9), kind=kOutput, calls=%fused_computation.56 | convolution fusion | flops 343933440 | bytes 9716736 | tf_op jit(solution)/shard_map/sub | solution.py:101
  70.4 4.3 %fusion.14 = bf16[2,512,4,80]{1,3,2,0:T(8,128)(2,1)S(1)} fusion(f32[2,4,512,512]{2,3,1,0:T(8,128)} %get-tuple-element.13, f32[2,4,512]{2,1,0:T(4,128)S(1)} %get-tuple-element.12, bf16[2,512,1,4,80]{1,0,4,3,2:T(2,128)(2,1)S(1)} %get-tuple-element.7), kind=kOutput, calls=%fused_computation.25 | convolution fusion | flops 340066304 | bytes 9715712 | tf_op jit(solution)/shard_map/nhqk,nkhd->nqhd/dot_general | solution.py:103
  74.7 0.7 copy.45
  75.4 0.1 copy.57
  75.5 0.3 broadcast_in_dim.69
  75.8 0.0 copy-start.2
  75.8 0.0 copy-start.9
  75.8 0.0 copy-start.10
  75.9 27.3 %all_to_all.21 = bf16[4,1024,320]{1,2,0:T(8,128)(2,1)S(1)} all-to-all(bf16[4,1024,320]{1,2,0:T(8,128)(2,1)S(1)} %broadcast_in_dim.69), channel_id=1, replica_groups=mesh['dp'=128,'tensor'=4] {'tensor'}, dimensions={0} | all-to-all | bytes 5242880 | tf_op jit(solution)/shard_map/all_to_all | solution.py:20
  103.1 0.0 copy-done.2
  103.1 0.0 copy-done.9
  103.1 0.0 copy-done.10
  103.2 0.0 copy-start.7
  103.2 0.0 copy-start.8
  103.2 2.3 fusion.27
  105.5 6.7 %all_to_all.22 = f32[4,1,2048]{2,1,0:T(1,128)S(1)} all-to-all(f32[4,1,2048]{2,1,0:T(1,128)S(1)} %broadcast_in_dim.70), channel_id=1, replica_groups=mesh['dp'=128,'tensor'=4] {'tensor'}, dimensions={0} | all-to-all | bytes 65536 | tf_op jit(solution)/shard_map/all_to_all | solution.py:20
  112.2 0.0 copy-done.7
  112.2 0.0 copy-done.8
  112.3 2.4 %add_convert_fusion.1 = bf16[1024,320]{0,1:T(8,128)(2,1)} fusion(f32[1024,320]{0,1:T(8,128)} %get-tuple-element.14, f32[320]{0:T(512)S(1)} %copy-done.7, f32[320]{0:T(512)S(1)} %copy-done.8, f32[1024]{0:T(1024)S(1)} %get-tuple-element.11, f32[1024]{0:T(1024)S(1)} %get-tuple-element.10), kind=kLoop, calls=%fused_computation.23 | loop fusion | flops 1638400 | bytes 1976832 | tf_op jit(solution)/shard_map/convert_element_type | solution.py:121
  114.7 1.4 copy.47
  116.1 1.6 reshape.137
  117.7 0.0 copy-start.1
  117.7 50.8 %all-gather.2.cloned.1.call-done = bf16[4,320,4096]{1,0,2:T(4,128)(2,1)} async-done(((bf16[4,320,32]{1,0,2:T(4,128)(2,1)}), bf16[4,320,4096]{1,0,2:T(4,128)(2,1)}) %all-gather.2.cloned.1.call-update) | async-done | bytes 10485776 | tf_op jit(solution)/shard_map/all_gather | solution.py:153
  168.5 19.6 %copy.49 = bf16[4,320,4096]{2,1,0:T(8,128)(2,1)} copy(bf16[4,320,4096]{1,0,2:T(4,128)(2,1)} %all-gather.2.cloned.1.call-done) | data formatting | bytes 20971520 | tf_op jit(solution)/shard_map/all_gather | solution.py:153
  188.1 0.0 copy-done.1
  188.1 8.1 %convolution_convert_fusion = bf16[256,4096]{1,0:T(8,128)(2,1)} fusion(bf16[256,1280]{1,0:T(8,128)(2,1)S(1)} %copy-done.1, bf16[1280,4096]{1,0:T(8,128)(2,1)} %bitcast.50), kind=kOutput, calls=%fused_computation.13 | convolution fusion | flops 2685403136 | bytes 13238272 | tf_op jit(solution)/shard_map/dot_general | solution.py:154
  196.2 4.4 %all-to-all-start.3 = ((bf16[4,64,4096]{2,1,0:T(8,128)(2,1)}), bf16[4,64,4096]{2,1,0:T(8,128)(2,1)}, u32[]{:S(2)}, u32[]{:S(2)}) async-start(bf16[4,64,4096]{2,1,0:T(8,128)(2,1)} %bitcast.55), calls=%async_computation.3 | async-start | bytes 4194304 | tf_op jit(solution)/shard_map/all_to_all | solution.py:54
  200.6 0.0 copy-start.3
  200.7 0.1 fusion.22
  200.8 26.1 %all-to-all-done.3 = bf16[4,64,4096]{2,1,0:T(8,128)(2,1)} async-done(((bf16[4,64,4096]{2,1,0:T(8,128)(2,1)}), bf16[4,64,4096]{2,1,0:T(8,128)(2,1)}, u32[]{:S(2)}, u32[]{:S(2)}) %all-to-all-start.3) | async-done | bytes 2097184 | tf_op jit(solution)/shard_map/all_to_all | solution.py:54
  226.9 2.1 convert_reduce_fusion.1
  228.9 0.0 copy-done.3
  228.9 0.9 fusion.18
  (8 shorter events, 0.1 us)
Async XLA Ops:
  6.5 42.9 %copy-start = (bf16[1280,3,320]{0,2,1:T(8,128)(2,1)S(1)}, bf16[1280,3,320]{0,2,1:T(8,128)(2,1)}, u32[]{:S(2)}) copy-start(bf16[1280,3,320]{0,2,1:T(8,128)(2,1)} %param.16) | copy-start | bytes 7372804
  6.5 162.0 %all-gather.2.cloned.1.call-start = ((), (), s32[]{:S(2)}) async-start(), calls=%async_computation.4 | async-start | bytes 12681216 | tf_op jit(solution)/shard_map/all_gather | solution.py:153
  11.2 5.0 %copy-start.6 = (f32[3,320]{1,0:T(4,128)S(1)}, f32[3,320]{1,0:T(4,128)}, u32[]{:S(2)}) copy-start(f32[3,320]{1,0:T(4,128)} %param.17) | copy-start | bytes 11524
  11.2 5.1 %copy-start.4 = (f32[1280]{0:T(1024)S(1)}, f32[1280]{0:T(1024)}, u32[]{:S(2)}) copy-start(f32[1280]{0:T(1024)} %param.14) | copy-start | bytes 15364
  11.2 5.1 %copy-start.5 = (f32[1280]{0:T(1024)S(1)}, f32[1280]{0:T(1024)}, u32[]{:S(2)}) copy-start(f32[1280]{0:T(1024)} %param.15) | copy-start | bytes 15364
  11.2 5.2 %copy-start.11 = (s32[256]{0:T(256)S(1)}, s32[256]{0:T(256)}, u32[]{:S(2)}) copy-start(s32[256]{0:T(256)} %param.13) | copy-start | bytes 3076
  11.2 31.2 %all-to-all-start = ((bf16[4,1024,320]{1,2,0:T(8,128)(2,1)}), bf16[4,1024,320]{1,2,0:T(8,128)(2,1)}, u32[]{:S(2)}, u32[]{:S(2)}) async-start(bf16[4,1024,320]{1,2,0:T(8,128)(2,1)} %broadcast_in_dim.40), calls=%async_computation | async-start | bytes 5242880 | tf_op jit(solution)/shard_map/all_to_all | solution.py:20
  75.8 27.3 %copy-start.2 = (bf16[1024,320]{0,1:T(8,128)(2,1)S(1)}, bf16[1024,320]{0,1:T(8,128)(2,1)}, u32[]{:S(2)}) copy-start(bf16[1024,320]{0,1:T(8,128)(2,1)} %param.12) | copy-start | bytes 1966084
  75.8 27.3 %copy-start.9 = (bf16[1280,320]{0,1:T(8,128)(2,1)S(1)}, bf16[1280,320]{0,1:T(8,128)(2,1)}, u32[]{:S(2)}) copy-start(bf16[1280,320]{0,1:T(8,128)(2,1)} %param.18) | copy-start | bytes 2457604
  75.8 27.3 %copy-start.10 = (f32[320]{0:T(512)S(1)}, f32[320]{0:T(512)}, u32[]{:S(2)}) copy-start(f32[320]{0:T(512)} %param.19) | copy-start | bytes 3844
  103.2 9.1 %copy-start.7 = (f32[320]{0:T(512)S(1)}, f32[320]{0:T(512)}, u32[]{:S(2)}) copy-start(f32[320]{0:T(512)} %param.21) | copy-start | bytes 3844
  103.2 9.1 %copy-start.8 = (f32[320]{0:T(512)S(1)}, f32[320]{0:T(512)}, u32[]{:S(2)}) copy-start(f32[320]{0:T(512)} %param.20) | copy-start | bytes 3844
  117.7 70.4 %copy-start.1 = (bf16[256,1280]{1,0:T(8,128)(2,1)S(1)}, bf16[256,1280]{1,0:T(8,128)(2,1)}, u32[]{:S(2)}) copy-start(bf16[256,1280]{1,0:T(8,128)(2,1)} %reshape.137) | copy-start | bytes 1966084
  196.2 30.7 %all-to-all-start.3 = ((bf16[4,64,4096]{2,1,0:T(8,128)(2,1)}), bf16[4,64,4096]{2,1,0:T(8,128)(2,1)}, u32[]{:S(2)}, u32[]{:S(2)}) async-start(bf16[4,64,4096]{2,1,0:T(8,128)(2,1)} %bitcast.55), calls=%async_computation.3 | async-start | bytes 4194304 | tf_op jit(solution)/shard_map/all_to_all | solution.py:54
  200.6 28.3 %copy-start.3 = (f32[4096]{0:T(1024)S(1)}, f32[4096]{0:T(1024)}, u32[]{:S(2)}) copy-start(f32[4096]{0:T(1024)} %param.23) | copy-start | bytes 49156
Sparse Core Ops, SparseCore 0:
  10.5 157.9 all-gather.1
where the time goes:
time: 238 us; the launch traced here: 237 us
  waiting for transfers between devices  103 us (43%)
  local copies, waits for them, and re-layouts  37.9 us (16%)
  blocking collectives  34 us (14%)
  matrix products  26.4 us (11%)
  between operations  13.6 us (6%)
  other arithmetic  12.7 us (5%)
  starting transfers between devices  9.42 us (4%)
    all_gather x1, waiting for transfers between devices, per_device(): piece = lax.all_gather(merger_weight, 'dp', axis=2, tiled=True)  50.8 us
    all_to_all x2, blocking collectives, sent_to_all(): return lax.all_to_all(copies, axis, split_axis=0, concat_axis=0, tiled=True)  34 us
    all_to_all x1, waiting for transfers between devices, summed_on_arrival(): lax.all_to_all(pieces, axis, split_axis=0, concat_axis=0, tiled=True)  26.1 us
    all_to_all x1, waiting for transfers between devices, sent_to_all(): return lax.all_to_all(copies, axis, split_axis=0, concat_axis=0, tiled=True)  25.8 us
    all_gather x1, local copies, waits for them, and re-layouts, per_device(): piece = lax.all_gather(merger_weight, 'dp', axis=2, tiled=True)  19.6 us
    dot_general x1, matrix products, per_device(): jnp.dot(merged, piece.reshape(-1, piece.shape[2]), preferred_element_type...  8.1 us
    sub x1, matrix products, encode(): raised = jnp.exp(scores - highest)  7.86 us
    reshape x1, local copies, waits for them, and re-layouts, encode(): projected = projected.reshape(number, TILE, 3, local_heads, head_size)  5.76 us
  transfers between devices with their start and end apart: 3, of which 3 were waited for; matrix products, arithmetic and copies ran while one was open for 19% of the time, Pallas kernels for 0%

commit v1 on v0

v1 whole, which is shorter than its diff:
```python
import functools
import math

import jax
import jax.numpy as jnp
from jax import lax
from jax.experimental import pallas as pl
from jax.experimental.pallas import tpu as pltpu
from jax.sharding import PartitionSpec as P

D = 1280
HEADS = 16
TILE = 512
NX = 4
NY = 4
NZ = 16
BLOCK = D // NX
HEAD = D // HEADS
LOCAL_HEADS = BLOCK // HEAD
LLMW = 4096
MROWS = TILE // 4
HALF = MROWS // 2
QUARTER = HALF // 2
ZCOLS = LLMW // NZ
PHASES = NZ // 2

EPS = 1e-06
MASKED = -1e30
MESH = pl.DeviceIdType.MESH
F32 = jnp.float32
BF16 = jnp.bfloat16
CHUNK = 80

NT = (((1,), (1,)), ((), ()))
TN = (((0,), (0,)), ((), ()))


def kernel(
    counts,
    patches,
    in_w_hbm,
    out_w_hbm,
    vec,
    mw,
    mbias,
    out,
    slot0,
    slot1,
    xbuf,
    hbuf,
    in_w,
    out_w,
    vt,
    normed,
    proj,
    stat,
    resid,
    wbuf,
    merged,
    pbuf,
    xpb,
    rel_a,
    rel_b,
    rs_a,
    rs_b,
    fa1,
    fa2,
    fb1,
    fb2,
    local_sem,
    part_send,
    part_recv,
    g_send,
    g_recv,
    h_send,
    h_recv,
    st_send,
    st_recv,
    y_send,
    y_recv,
    up_send,
    up_recv,
    dn_send,
    dn_recv,
    pf_send,
    pf_recv,
    rs_send,
    rs_recv,
):
    rank = lax.axis_index("dp")
    t = lax.axis_index("tensor")
    c = lax.rem(rank, 2)
    y = lax.rem(rank // 2, NY)
    z = rank // (2 * NY)
    partner = rank + 1 - 2 * c
    right = lax.rem(t + 1, NX)
    left = lax.rem(t + NX - 1, NX)
    across = lax.rem(t + 2, NX)

    def zwrap(k):
        return lax.rem(k + NZ, NZ)

    def rank_of(zz, yy):
        return (zz * NY + yy) * 2 + c

    up = rank_of(zwrap(z + 1), y)
    down = rank_of(zwrap(z - 1), y)

    peers = [(rank, right), (rank, left), (partner, right), (partner, left), (rank, across), (partner, t)]
    peers += [(rank_of(z, lax.rem(y + dy, NY)), t) for dy in range(1, NY)]
    peers += [(up, t), (down, t)]
    barrier = pltpu.get_barrier_semaphore()
    for peer in peers:
        pl.semaphore_signal(barrier, inc=1, device_id=peer, device_id_type=MESH)
    pl.semaphore_wait(barrier, len(peers))

    def remote(src, dst, send, recv, device):
        return pltpu.make_async_remote_copy(
            src_ref=src, dst_ref=dst, send_sem=send, recv_sem=recv, device_id=device, device_id_type=MESH
        )

    swap = remote(patches.at[:, pl.ds(TILE, TILE)], slot1, part_send, part_recv, (partner, t))
    swap.start()
    first = pltpu.make_async_copy(patches.at[:, pl.ds(0, TILE)], slot0, local_sem.at[0])
    first.start()
    mine = pltpu.make_async_copy(mw, wbuf.at[z, y, c], local_sem.at[1])
    mine.start()
    y_copies = []
    for dy in range(1, NY):
        copy = remote(
            mw,
            wbuf.at[z, y, c],
            y_send.at[dy - 1],
            y_recv.at[dy - 1],
            (rank_of(z, lax.rem(y + dy, NY)), t),
        )
        copy.start()
        y_copies.append(copy)
    win_copy = pltpu.make_async_copy(in_w_hbm, in_w, local_sem.at[2])
    win_copy.start()
    wout_copy = pltpu.make_async_copy(out_w_hbm, out_w, local_sem.at[3])
    wout_copy.start()
    vt[...] = jnp.transpose(vec[...])

    def sub(buf, owner, h):
        return buf.at[pl.ds(pl.multiple_of(owner * BLOCK + h * HEAD, 16), HEAD)]

    def gather_copy(buf, send, recv, owner, h, way, hop):
        ref = sub(buf, owner, h)
        return remote(ref, ref, send.at[way, hop, h], recv.at[way, hop, h], (rank, right if way == 0 else left))

    def gather_wait(buf, send, recv, h, way, hop):
        owner = lax.rem(t + (NX - 1 - hop if way == 0 else 1 + hop), NX)
        ref = sub(buf, owner, h)
        remote(ref, ref, send.at[way, hop, h], recv.at[way, hop, h], (rank, right)).wait_recv()

    def own_send(buf, send, recv, h, way):
        gather_copy(buf, send, recv, t, h, way, 0).start()

    def forward(buf, send, recv, h):
        way = h % 2
        gather_wait(buf, send, recv, h, way, 0)
        owner = left if way == 0 else right
        gather_copy(buf, send, recv, owner, h, way, 1).start()

    def finish_gather(buf, send, recv):
        for h in range(LOCAL_HEADS):
            gather_wait(buf, send, recv, h, 1 - h % 2, 0)
        for h in range(LOCAL_HEADS):
            gather_wait(buf, send, recv, h, h % 2, 1)

    def drain_gather(buf, send, recv):
        for h in range(LOCAL_HEADS):
            for way in range(2):
                gather_copy(buf, send, recv, t, h, way, 0).wait_send()
            gather_copy(buf, send, recv, t, h, h % 2, 1).wait_send()

    def zblock(zz):
        return wbuf.at[zz, :, c]

    def up_copy(s):
        ref = zblock(zwrap(z - (s - 1)))
        return remote(ref, ref, up_send.at[s - 1], up_recv.at[s - 1], (up, t))

    def down_copy(s):
        ref = zblock(zwrap(z + (s - 1)))
        return remote(ref, ref, dn_send.at[s - 1], dn_recv.at[s - 1], (down, t))

    def hand_over(index, zz):
        ref = zblock(zz)
        return remote(ref, ref, pf_send.at[index], pf_recv.at[index], (partner, t))

    def hand_wait(index, zz):
        ref = wbuf.at[zz, :, 1 - c]
        remote(ref, ref, pf_send.at[index], pf_recv.at[index], (partner, t)).wait_recv()

    def weights_begin():
        mine.wait()
        for dy in range(1, NY):
            ref = wbuf.at[z, lax.rem(y + NY - dy, NY), c]
            remote(ref, ref, y_send.at[dy - 1], y_recv.at[dy - 1], (rank, t)).wait_recv()
        up_copy(1).start()
        down_copy(1).start()
        hand_over(0, z).start()

    def weights_step(s):
        from_below, from_above = zwrap(z - s), zwrap(z + s)
        ref = zblock(from_below)
        remote(ref, ref, up_send.at[s - 1], up_recv.at[s - 1], (up, t)).wait_recv()
        if s + 1 <= PHASES:
            up_copy(s + 1).start()
        if s < PHASES:
            ref = zblock(from_above)
            remote(ref, ref, dn_send.at[s - 1], dn_recv.at[s - 1], (down, t)).wait_recv()
            if s + 1 < PHASES:
                down_copy(s + 1).start()
        hand_over(2 * s - 1, from_below).start()
        if s < PHASES:
            hand_over(2 * s, from_above).start()

    own0 = counts[2 * rank]
    other1 = counts[2 * partner + 1]
    tile_count = jnp.where(own0 > 0, own0, other1)
    first.wait()
    swap.wait_recv()

    def choose(i, carry):
        rows = pl.ds(pl.multiple_of(i * CHUNK, 16), CHUNK)
        pick = jnp.full((CHUNK, TILE), own0, jnp.int32) > 0
        value = jnp.where(pick, slot0[rows, :].astype(F32), slot1[rows, :].astype(F32))
        xbuf[pl.ds(pl.multiple_of(t * BLOCK + i * CHUNK, 16), CHUNK), :] = value.astype(BF16)
        return carry

    lax.fori_loop(0, BLOCK // CHUNK, choose, 0)
    for h in (0, 2, 1, 3):
        own_send(xbuf, g_send, g_recv, h, 0)
        own_send(xbuf, g_send, g_recv, (h + 1) if h % 2 == 0 else (h - 1), 1)
    weights_begin()
    for h in range(LOCAL_HEADS):
        forward(xbuf, g_send, g_recv, h)
    finish_gather(xbuf, g_send, g_recv)
    weights_step(1)

    def total_of(i, acc):
        x = xbuf[pl.ds(pl.multiple_of(i * CHUNK, 16), CHUNK), :].astype(F32)
        return acc + jnp.sum(x, axis=0, keepdims=True)

    zero_row = jnp.zeros((1, TILE), F32)
    mean = lax.fori_loop(0, D // CHUNK, total_of, zero_row) * (1.0 / D)

    def spread_of(i, acc):
        x = xbuf[pl.ds(pl.multiple_of(i * CHUNK, 16), CHUNK), :].astype(F32) - mean
        return acc + jnp.sum(x * x, axis=0, keepdims=True)

    spread = lax.fori_loop(0, D // CHUNK, spread_of, zero_row) * (1.0 / D)
    inv = lax.rsqrt(spread + EPS)

    def normalise(i, carry):
        rows = pl.ds(pl.multiple_of(i * CHUNK, 16), CHUNK)
        x = xbuf[rows, :].astype(F32)
        gain = vt[rows, 0:1]
        shift = vt[rows, 1:2]
        normed[rows, :] = ((x - mean) * inv * gain + shift).astype(BF16)
        return carry

    lax.fori_loop(0, D // CHUNK, normalise, 0)

    win_copy.wait()
    for part in range(3):
        rows = pl.ds(part * BLOCK, BLOCK)
        got = jnp.dot(in_w[rows, :], normed[...], preferred_element_type=F32)
        proj[rows, :] = (got + vt[rows, 2:3]).astype(BF16)
    weights_step(2)

    scale = 1.0 / math.sqrt(HEAD)

    def attend(h):
        q_rows = pl.ds(h * HEAD, HEAD)
        k_rows = pl.ds(BLOCK + h * HEAD, HEAD)
        v_rows = pl.ds(2 * BLOCK + h * HEAD, HEAD)
        live = lax.broadcasted_iota(jnp.int32, (TILE, TILE // 2), 0) < tile_count

        def columns(i, carry):
            cols = pl.ds(pl.multiple_of(i * (TILE // 2), 128), TILE // 2)
            scores = lax.dot_general(proj[k_rows, :], proj[q_rows, cols], TN, preferred_element_type=F32)
            scores = jnp.where(live, scores * scale, MASKED)
            highest = jnp.max(scores, axis=0, keepdims=True)
            raised = jnp.exp(scores - highest)
            weights = (raised * (1.0 / jnp.sum(raised, axis=0, keepdims=True))).astype(BF16)
            got = jnp.dot(proj[v_rows, :], weights, preferred_element_type=F32)
            hbuf[pl.ds(pl.multiple_of(t * BLOCK + h * HEAD, 16), HEAD), cols] = got.astype(BF16)
            return carry

        lax.fori_loop(0, 2, columns, 0)

    for h in range(LOCAL_HEADS):
        attend(h)
        own_send(hbuf, h_send, h_recv, h, 0)
        own_send(hbuf, h_send, h_recv, h, 1)
        if h >= 2:
            forward(hbuf, h_send, h_recv, h - 2)
    forward(hbuf, h_send, h_recv, 2)
    forward(hbuf, h_send, h_recv, 3)
    weights_step(3)
    finish_gather(hbuf, h_send, h_recv)

    wout_copy.wait()
    got = jnp.dot(out_w[...], hbuf[...], preferred_element_type=F32)
    resid[...] = xbuf[pl.ds(pl.multiple_of(t * BLOCK, 16), BLOCK), :].astype(F32) + got + vt[0:BLOCK, 3:4]

    def sums_of(i, acc):
        x = resid[pl.ds(pl.multiple_of(i * CHUNK, 16), CHUNK), :]
        return acc[0] + jnp.sum(x, axis=0, keepdims=True), acc[1] + jnp.sum(x * x, axis=0, keepdims=True)

    row_sum, row_squares = lax.fori_loop(0, BLOCK // CHUNK, sums_of, (zero_row, zero_row))
    stat[3] = jnp.concatenate([row_sum, row_squares, jnp.zeros((6, TILE), F32)], axis=0)
    targets = (right, left, across)
    for k in range(3):
        remote(stat.at[3], stat.at[k], st_send.at[k], st_recv.at[k], (rank, targets[k])).start()
    weights_step(4)
    for k in range(3):
        remote(stat.at[3], stat.at[k], st_send.at[k], st_recv.at[k], (rank, targets[k])).wait_recv()
    sums = stat[0] + stat[1] + stat[2] + stat[3]
    row_mean = sums[0:1] * (1.0 / D)
    second = sums[1:2] * (1.0 / D)
    inv2 = lax.rsqrt(second - row_mean * row_mean + EPS)

    def encode(i, carry):
        rows = pl.ds(pl.multiple_of(i * CHUNK, 16), CHUNK)
        x = resid[rows, :]
        value = (x - row_mean) * inv2 * vt[rows, 4:5] + vt[rows, 5:6]
        proj[rows, :] = value.astype(BF16)
        return carry

    lax.fori_loop(0, BLOCK // CHUNK, encode, 0)
    pieces = []
    for j in range(4):
        chosen = (
            lax.broadcasted_iota(jnp.int32, (MROWS, TILE), 1)
            == 4 * lax.broadcasted_iota(jnp.int32, (MROWS, TILE), 0) + j
        )
        pick = jnp.where(chosen, 1.0, 0.0).astype(BF16)
        pieces.append(lax.dot_general(pick, proj[0:BLOCK, :], NT, preferred_element_type=F32))
    merged[...] = jnp.concatenate(pieces, axis=1).astype(BF16)

    same = pl.multiple_of(lax.rem(t, 2) * HALF, 16)
    other = pl.multiple_of(HALF - lax.rem(t, 2) * HALF, 16)
    upper = t // 2
    right_up, left_up = right // 2, left // 2
    right_rank = rank + (partner - rank) * right_up
    left_rank = rank + (partner - rank) * left_up

    def rs_copies(s):
        a_same, b_same = pl.ds(same, QUARTER), pl.ds(pl.multiple_of(same + QUARTER, 16), QUARTER)
        a_other, b_other = pl.ds(other, QUARTER), pl.ds(pl.multiple_of(other + QUARTER, 16), QUARTER)
        return (
            remote(pbuf.at[s, a_same], rel_a.at[s], rs_send.at[s, 0], rs_recv.at[s, 0], (rank, right)),
            remote(pbuf.at[s, b_same], rel_b.at[s], rs_send.at[s, 1], rs_recv.at[s, 1], (rank, left)),
            remote(pbuf.at[s, b_other], fb1.at[s], rs_send.at[s, 2], rs_recv.at[s, 2], (right_rank, right)),
            remote(pbuf.at[s, a_other], fa1.at[s], rs_send.at[s, 3], rs_recv.at[s, 3], (left_rank, left)),
            remote(rs_a.at[s], fa2.at[s], rs_send.at[s, 4], rs_recv.at[s, 4], (right_rank, right)),
            remote(rs_b.at[s], fb2.at[s], rs_send.at[s, 5], rs_recv.at[s, 5], (left_rank, left)),
            remote(pbuf.at[s, pl.ds(same, HALF)], xpb.at[s], rs_send.at[s, 6], rs_recv.at[s, 6], (partner, t)),
        )

    def z_of(s):
        return (zwrap(z - s), zwrap(z + s)) if s else (z, zwrap(z - PHASES))

    def project(s):
        for k, zz in enumerate(z_of(s)):
            part = wbuf[zz].reshape(ZCOLS, D)
            got = lax.dot_general(merged[...], part, NT, preferred_element_type=F32)
            pbuf[s, :, k * ZCOLS : (k + 1) * ZCOLS] = got.astype(BF16)
        copies = rs_copies(s)
        for k in (0, 1, 2, 3, 6):
            copies[k].start()

    def relay(s):
        copies = rs_copies(s)
        copies[0].wait_recv()
        own = pbuf[s, pl.ds(other, QUARTER), :].astype(F32)
        rs_a[s] = (rel_a[s].astype(F32) + own).astype(BF16)
        copies[4].start()
        copies[1].wait_recv()
        own = pbuf[s, pl.ds(pl.multiple_of(other + QUARTER, 16), QUARTER), :].astype(F32)
        rs_b[s] = (rel_b[s].astype(F32) + own).astype(BF16)
        copies[5].start()

    my_count = counts[2 * rank + upper]

    def collect(s):
        copies = rs_copies(s)
        for k in (2, 3, 4, 5, 6):
            copies[k].wait_recv()
        local = pbuf[s, pl.ds(same, HALF), :].astype(F32)
        passed = xpb[s].astype(F32)
        is_upper = jnp.full((HALF, 2 * ZCOLS), upper, jnp.int32) > 0
        total = jnp.where(is_upper, passed, local)
        top = fa1[s].astype(F32) + fa2[s].astype(F32)
        bottom = fb1[s].astype(F32) + fb2[s].astype(F32)
        total = total + jnp.concatenate([top, bottom], axis=0)
        row = lax.broadcasted_iota(jnp.int32, (HALF, ZCOLS), 0) + lax.rem(t, 2) * HALF
        keep = 4 * row < my_count
        for k, zz in enumerate(z_of(s)):
            cols = pl.ds(pl.multiple_of(zz * ZCOLS, 128), ZCOLS)
            value = total[:, k * ZCOLS : (k + 1) * ZCOLS] + mbias[:, cols]
            out[:, cols] = jnp.where(keep, value, 0.0).astype(BF16)

    hand_wait(0, z)
    order = (1, 2, 3, 4, 5, 6, 7, 0)
    for n, s in enumerate(order):
        if n + 5 <= PHASES:
            if n >= 1 or True:
                weights_step(n + 5)
        if s:
            hand_wait(2 * s - 1, zwrap(z - s))
            hand_wait(2 * s, zwrap(z + s))
        else:
            hand_wait(2 * PHASES - 1, zwrap(z - PHASES))
        project(s)
        if n >= 1:
            relay(order[n - 1])
        if n >= 3:
            collect(order[n - 3])
    relay(order[7])
    for n in (5, 6, 7):
        collect(order[n])

    swap.wait_send()
    for copy in y_copies:
        copy.wait_send()
    drain_gather(xbuf, g_send, g_recv)
    drain_gather(hbuf, h_send, h_recv)
    for k in range(3):
        remote(stat.at[3], stat.at[k], st_send.at[k], st_recv.at[k], (rank, targets[k])).wait_send()
    for s in range(1, PHASES + 1):
        up_copy(s).wait_send()
        if s < PHASES:
            down_copy(s).wait_send()
    for index in range(NZ):
        hand_over(index, z).wait_send()
    for s in range(PHASES):
        for copy in rs_copies(s):
            copy.wait_send()


def per_device(
    patches,
    counts,
    first_gain,
    first_shift,
    in_weight,
    in_bias,
    out_weight,
    out_bias,
    second_gain,
    second_shift,
    merger_weight,
    merger_bias,
):
    def padded(v):
        return jnp.pad(v.reshape(-1), (0, D - v.size))

    zero = jnp.zeros((D,), F32)
    vec = jnp.stack(
        [first_gain, first_shift, padded(in_bias), padded(out_bias), padded(second_gain), padded(second_shift), zero, zero]
    )
    mw = jnp.transpose(merger_weight, (2, 0, 1)).reshape(LLMW // 128, D)
    any_spec = pl.BlockSpec(memory_space=pl.ANY)
    vmem = pl.BlockSpec(memory_space=pltpu.VMEM)
    dma = pltpu.SemaphoreType.DMA
    return pl.pallas_call(
        kernel,
        out_shape=jax.ShapeDtypeStruct((HALF, LLMW), BF16),
        in_specs=[pl.BlockSpec(memory_space=pltpu.SMEM), any_spec, any_spec, any_spec, vmem, any_spec, vmem],
        out_specs=vmem,
        scratch_shapes=[
            pltpu.VMEM((BLOCK, TILE), BF16),
            pltpu.VMEM((BLOCK, TILE), BF16),
            pltpu.VMEM((D, TILE), BF16),
            pltpu.VMEM((D, TILE), BF16),
            pltpu.VMEM((3 * BLOCK, D), BF16),
            pltpu.VMEM((BLOCK, D), BF16),
            pltpu.VMEM((D, 8), F32),
            pltpu.VMEM((D, TILE), BF16),
            pltpu.VMEM((3 * BLOCK, TILE), BF16),
            pltpu.VMEM((4, 8, TILE), F32),
            pltpu.VMEM((BLOCK, TILE), F32),
            pltpu.VMEM((NZ, NY, 2, 32, D), BF16),
            pltpu.VMEM((MROWS, D), BF16),
            pltpu.VMEM((PHASES, MROWS, 2 * ZCOLS), BF16),
            pltpu.VMEM((PHASES, HALF, 2 * ZCOLS), BF16),
        ]
        + [pltpu.VMEM((PHASES, QUARTER, 2 * ZCOLS), BF16)] * 8
        + [
            dma((4,)),
            dma,
            dma,
            dma((2, 2, LOCAL_HEADS)),
            dma((2, 2, LOCAL_HEADS)),
            dma((2, 2, LOCAL_HEADS)),
            dma((2, 2, LOCAL_HEADS)),
            dma((3,)),
            dma((3,)),
            dma((NY - 1,)),
            dma((NY - 1,)),
            dma((PHASES,)),
            dma((PHASES,)),
            dma((PHASES,)),
            dma((PHASES,)),
            dma((NZ,)),
            dma((NZ,)),
            dma((PHASES, 7)),
            dma((PHASES, 7)),
        ],
        compiler_params=pltpu.CompilerParams(
            collective_id=0, has_side_effects=True, vmem_limit_bytes=60 * 1024 * 1024
        ),
        name="vision_block",
    )(
        counts,
        patches.T,
        jnp.transpose(in_weight, (1, 2, 0)).reshape(3 * BLOCK, D),
        out_weight.T,
        vec,
        mw,
        merger_bias.reshape(1, LLMW),
    )


def solution(mesh):
    return jax.shard_map(
        per_device,
        mesh=mesh,
        in_specs=(
            P("dp", "tensor"),
            P(),
            P(),
            P(),
            P(None, None, "tensor"),
            P(None, "tensor"),
            P(None, "tensor"),
            P("tensor"),
            P("tensor"),
            P("tensor"),
            P(None, "tensor", "dp"),
            P(),
        ),
        out_specs=P(("dp", "tensor"), None),
        check_vma=False,
    )
```

time: 238 us -> 121 us (0.51)
  the two profiles are of different devices: /device:TPU:1 before, /device:TPU:18 now
where the time goes in v1:
time: 121 us; the launch traced here: 120 us
  Pallas kernels  112 us (93%)
  local copies, waits for them, and re-layouts  8.5 us (7%)
    pallas_call x1, Pallas kernels, per_device(): pl.pallas_call(kernel, out_shape=jax.ShapeDtypeStruct((HALF, LLMW), BF16)...  112 us

profile of v1, /device:TPU:18, one launch (start us, length us, event | category | flops | bytes accessed | tf_op | source)
XLA Modules:
  0.0 120.3 jit_solution(657595140069647435)
XLA Ops:
  0.0 0.8 reshape.13
  0.8 0.7 stack.24
  1.5 0.7 stack.25
  2.2 0.7 pad.15
  2.9 0.7 pad.16
  3.6 0.7 pad.17
  4.3 0.7 stack.31.vec
  4.9 0.9 copy.13
  5.9 0.8 reshape.14.mw
  6.6 111.8 %vision_block.1 = bf16[64,4096]{1,0:T(8,128)(2,1)} custom-call(s32[256]{0:T(256)} %counts.1, bf16[320,1024]{1,0:T(8,128)(2,1)} %bitcast.9, bf16[960,1280]{1,0:T(8,128)(2,1)} %bitcast.7, bf16[320,1280]{1,0:T(8,128)(2,1)} %bitcast.8, f32[8,1280]{1,0:T(8,128)} %stack.31.vec, bf16[32,1280]{1,0:T(8,128)(2,1)} %reshape.14.mw, f32[1,4096]{1,0:T(1,128)} %bitcast.11), custom_call_target="tpu_custom_call" | custom-call | tf_op jit(solution)/shard_map/vision_block/pallas_call | solution.py:472
  118.5 1.9 %copy.15 = bf16[64,4096]{1,0:T(8,128)(2,1)} copy(bf16[64,4096]{1,0:T(8,128)(2,1)} %vision_block.1) | data formatting | bytes 1048576
  (6 shorter events, 0.0 us)

commit v2 on v1

v2 whole, which is shorter than its diff:
```python
import functools
import math

import jax
import jax.numpy as jnp
from jax import lax
from jax.experimental import pallas as pl
from jax.experimental.pallas import tpu as pltpu
from jax.sharding import PartitionSpec as P

D = 1280
HEADS = 16
TILE = 512
NX = 4
NY = 4
NZ = 16
BLOCK = D // NX
HEAD = D // HEADS
LOCAL_HEADS = BLOCK // HEAD
LLMW = 4096
MROWS = TILE // 4
HALF = MROWS // 2
QUARTER = HALF // 2
ZCOLS = LLMW // NZ
PHASES = NZ // 2

EPS = 1e-06
MASKED = -1e30
MESH = pl.DeviceIdType.MESH
F32 = jnp.float32
BF16 = jnp.bfloat16
CHUNK = 80
SPLIT = 384

NT = (((1,), (1,)), ((), ()))
TN = (((0,), (0,)), ((), ()))


def kernel(
    counts_hbm,
    patches,
    in_w_hbm,
    out_w_hbm,
    gain1,
    shift1,
    in_bias,
    out_bias,
    gain2,
    shift2,
    mw_hbm,
    mbias_hbm,
    out,
    slot0,
    slot1,
    xbuf,
    hbuf,
    in_w,
    out_w,
    vec,
    vec2,
    in_b,
    vt,
    vt2,
    vt3,
    mw,
    mbias,
    normed,
    proj,
    stat,
    resid,
    wbuf,
    merged,
    pbuf,
    xpb,
    rel_a,
    rel_b,
    rs_a,
    rs_b,
    fa1,
    fa2,
    fb1,
    fb2,
    obuf,
    counts,
    local_sem,
    out_sem,
    part_send,
    part_recv,
    g_send,
    g_recv,
    h_send,
    h_recv,
    st_send,
    st_recv,
    ya_send,
    ya_recv,
    yb_send,
    yb_recv,
    za_send,
    za_recv,
    zb_send,
    zb_recv,
    pf_send,
    pf_recv,
    rs_send,
    rs_recv,
):
    rank = lax.axis_index("dp")
    t = lax.axis_index("tensor")
    c = lax.rem(rank, 2)
    y = lax.rem(rank // 2, NY)
    z = rank // (2 * NY)
    partner = rank + 1 - 2 * c
    right = lax.rem(t + 1, NX)
    left = lax.rem(t + NX - 1, NX)
    across = lax.rem(t + 2, NX)

    def zwrap(k):
        return lax.rem(k + NZ, NZ)

    def rank_of(zz, yy):
        return (zz * NY + yy) * 2 + c

    up = rank_of(zwrap(z + 1), y)
    down = rank_of(zwrap(z - 1), y)

    peers = [(rank, right), (rank, left), (partner, right), (partner, left), (rank, across), (partner, t)]
    peers += [(rank_of(z, lax.rem(y + dy, NY)), t) for dy in range(1, NY)]
    peers += [(up, t), (down, t)]
    barrier = pltpu.get_barrier_semaphore()
    for peer in peers:
        pl.semaphore_signal(barrier, inc=1, device_id=peer, device_id_type=MESH)

    def load(src, dst, index):
        copy = pltpu.make_async_copy(src, dst, local_sem.at[index])
        copy.start()
        return copy

    mw_copy = load(mw_hbm, mw, 0)
    first = load(patches.at[:, pl.ds(0, TILE)], slot0, 1)
    counted = load(counts_hbm, counts, 15)
    small = [load(gain1, vec.at[0], 2), load(shift1, vec.at[1], 3)]
    small += [load(in_bias, in_b, 4)]
    small += [load(out_bias, vec2.at[3], 7), load(gain2, vec2.at[4], 8)]
    small += [load(shift2, vec2.at[5], 9), load(mbias_hbm, mbias.at[0], 10)]
    win_copies = [load(in_w_hbm.at[k], in_w.at[:, k], 11 + k) for k in range(3)]
    wout_copy = load(out_w_hbm, out_w, 14)
    mw_copy.wait()
    wbuf[z, y, c] = jnp.concatenate([mw[j] for j in range(4)], axis=1)
    for copy in small:
        copy.wait()
    vt[...] = jnp.transpose(vec[...])
    vt2[...] = jnp.transpose(vec2[...])
    vt3[...] = jnp.transpose(jnp.concatenate([in_b[...], jnp.zeros((5, BLOCK), F32)], axis=0))

    pl.semaphore_wait(barrier, len(peers))

    def remote(src, dst, send, recv, device):
        return pltpu.make_async_remote_copy(
            src_ref=src, dst_ref=dst, send_sem=send, recv_sem=recv, device_id=device, device_id_type=MESH
        )

    def send(*args):
        copy = remote(*args)
        copy.start()

    swap = remote(patches.at[:, pl.ds(TILE, TILE)], slot1, part_send, part_recv, (partner, t))
    swap.start()

    def sub(buf, owner, h):
        return buf.at[pl.ds(pl.multiple_of(owner * BLOCK + h * HEAD, 16), HEAD)]

    def gather_copy(buf, send, recv, owner, h, way, hop):
        ref = sub(buf, owner, h)
        return remote(ref, ref, send, recv.at[way, hop, h], (rank, right if way == 0 else left))

    def gather_wait(buf, send, recv, h, way, hop):
        owner = lax.rem(t + (NX - 1 - hop if way == 0 else 1 + hop), NX)
        ref = sub(buf, owner, h)
        remote(ref, ref, send, recv.at[way, hop, h], (rank, right)).wait_recv()

    def own_send(buf, send, recv, h, way):
        copy = gather_copy(buf, send, recv, t, h, way, 0)
        copy.start()

    def forward(buf, send, recv, h):
        way = h % 2
        gather_wait(buf, send, recv, h, way, 0)
        owner = left if way == 0 else right
        copy = gather_copy(buf, send, recv, owner, h, way, 1)
        copy.start()

    def near_wait(buf, send, recv):
        for h in range(LOCAL_HEADS):
            gather_wait(buf, send, recv, h, 1 - h % 2, 0)

    def far_wait(buf, send, recv):
        for h in range(LOCAL_HEADS):
            gather_wait(buf, send, recv, h, h % 2, 1)

    half_a, half_b = pl.ds(0, SPLIT), pl.ds(SPLIT, D - SPLIT)

    def arrived(ref, recv):
        remote(ref, ref, part_send, recv, (partner, t)).wait_recv()

    def z_step(k):
        for way, device in ((0, up), (1, down)):
            if k > PHASES - way:
                continue
            zz = zwrap(z - (k - 1)) if way == 0 else zwrap(z + (k - 1))
            ref = wbuf.at[zz, :, c, :, half_a]
            send(ref, ref, za_send, za_recv.at[way, k - 1], (device, t))

    def z_step_b(k):
        for way, device in ((0, up), (1, down)):
            if k > PHASES - way:
                continue
            zz = zwrap(z - (k - 1)) if way == 0 else zwrap(z + (k - 1))
            ref = wbuf.at[zz, y, c, :, half_b]
            send(ref, ref, zb_send, zb_recv.at[way, k - 1], (device, t))

    def blocks_of(k):
        if k == 0:
            return ((0, z),)
        if k == PHASES:
            return ((2 * PHASES - 1, zwrap(z - PHASES)),)
        return ((2 * k - 1, zwrap(z - k)), (2 * k, zwrap(z + k)))

    def y_block(zz, dy):
        return wbuf.at[zz, lax.rem(y + NY - dy, NY), c, :, half_b]

    def y_peer(dy):
        return (rank_of(z, lax.rem(y + dy, NY)), t)

    def y_send_b(k):
        for index, zz in blocks_of(k):
            ref = y_block(zz, 0)
            for dy in (1, 3):
                send(ref, ref, yb_send, yb_recv.at[index, dy - 1], y_peer(dy))

    def y_forward(k):
        for turn, (index, zz) in enumerate(blocks_of(k)):
            arrived(y_block(zz, 1), yb_recv.at[index, 0])
            arrived(y_block(zz, 3), yb_recv.at[index, 2])
            dy = 1 if turn == 0 else 3
            ref = y_block(zz, dy)
            send(ref, ref, yb_send, yb_recv.at[index, 1], y_peer(dy))

    def hand_over(k):
        for index, zz in blocks_of(k):
            arrived(y_block(zz, 2), yb_recv.at[index, 1])
            ref = wbuf.at[zz, :, c]
            send(ref, ref, pf_send, pf_recv.at[index], (partner, t))

    def hand_wait(k):
        for index, zz in blocks_of(k):
            arrived(wbuf.at[zz, :, 1 - c], pf_recv.at[index])

    def weights_begin():
        ref = wbuf.at[z, y, c, :, half_a]
        for dy in (1, 3, 2):
            send(ref, ref, ya_send, ya_recv.at[dy - 1], (rank_of(z, lax.rem(y + dy, NY)), t))
        z_step_b(1)
        y_send_b(0)

    def weights_first():
        for dy in range(1, NY):
            arrived(wbuf.at[z, lax.rem(y + NY - dy, NY), c, :, half_a], ya_recv.at[dy - 1])
        z_step(1)

    def weights_step(k):
        if k <= PHASES:
            for way, (index, zz) in enumerate(blocks_of(k)):
                arrived(wbuf.at[zz, y, c, :, half_b], zb_recv.at[way, k - 1])
                arrived(wbuf.at[zz, :, c, :, half_a], za_recv.at[way, k - 1])
            z_step(k + 1)
            z_step_b(k + 1)
            y_send_b(k)
        if k - 1 <= PHASES:
            y_forward(k - 1)
        if k >= 2:
            hand_over(k - 2)

    counted.wait()
    own0 = counts[2 * rank]
    other1 = counts[2 * partner + 1]
    tile_count = jnp.where(own0 > 0, own0, other1)
    weights_begin()
    first.wait()
    swap.wait_recv()

    def choose(i, carry):
        rows = pl.ds(pl.multiple_of(i * CHUNK, 16), CHUNK)
        pick = jnp.full((CHUNK, TILE), own0, jnp.int32) > 0
        value = jnp.where(pick, slot0[rows, :].astype(F32), slot1[rows, :].astype(F32))
        xbuf[pl.ds(pl.multiple_of(t * BLOCK + i * CHUNK, 16), CHUNK), :] = value.astype(BF16)
        return carry

    lax.fori_loop(0, BLOCK // CHUNK, choose, 0)
    for h in (0, 2, 1, 3):
        own_send(xbuf, g_send, g_recv, h, 0)
        own_send(xbuf, g_send, g_recv, (h + 1) if h % 2 == 0 else (h - 1), 1)
    weights_first()

    def block_stats(owner):
        base = owner * BLOCK

        def total_of(i, acc):
            x = xbuf[pl.ds(pl.multiple_of(base + i * CHUNK, 16), CHUNK), :].astype(F32)
            return acc + jnp.sum(x, axis=0, keepdims=True)

        centre = lax.fori_loop(0, BLOCK // CHUNK, total_of, zero_row) * (1.0 / BLOCK)

        def spread_of(i, acc):
            x = xbuf[pl.ds(pl.multiple_of(base + i * CHUNK, 16), CHUNK), :].astype(F32) - centre
            return acc + jnp.sum(x * x, axis=0, keepdims=True)

        return centre, lax.fori_loop(0, BLOCK // CHUNK, spread_of, zero_row)

    zero_row = jnp.zeros((1, TILE), F32)
    stats = [block_stats(t)]
    for h in range(LOCAL_HEADS):
        forward(xbuf, g_send, g_recv, h)
    weights_step(1)
    near_wait(xbuf, g_send, g_recv)
    stats += [block_stats(left), block_stats(right)]
    weights_step(2)
    far_wait(xbuf, g_send, g_recv)
    stats += [block_stats(across)]
    mean = (stats[0][0] + stats[1][0] + stats[2][0] + stats[3][0]) * (1.0 / NX)
    spread = zero_row
    for centre, squares in stats:
        off = centre - mean
        spread = spread + squares + float(BLOCK) * (off * off)
    inv = lax.rsqrt(spread * (1.0 / D) + EPS)

    def normalise(i, carry):
        rows = pl.ds(pl.multiple_of(i * CHUNK, 16), CHUNK)
        x = xbuf[rows, :].astype(F32)
        gain = vt[rows, 0:1]
        shift = vt[rows, 1:2]
        normed[rows, :] = ((x - mean) * inv * gain + shift).astype(BF16)
        return carry

    lax.fori_loop(0, D // CHUNK, normalise, 0)
    weights_step(3)

    for copy in win_copies:
        copy.wait()
    scale = 1.0 / math.sqrt(HEAD)

    def attend(h):
        got = jnp.dot(in_w[h].reshape(3 * HEAD, D), normed[...], preferred_element_type=F32)
        bias = jnp.concatenate([vt3[h * HEAD : (h + 1) * HEAD, k : k + 1] for k in range(3)], axis=0)
        proj[0 : 3 * HEAD, :] = (got + bias).astype(BF16)
        live = lax.broadcasted_iota(jnp.int32, (TILE, TILE // 2), 0) < tile_count

        def columns(i, carry):
            cols = pl.ds(pl.multiple_of(i * (TILE // 2), 128), TILE // 2)
            scores = lax.dot_general(
                proj[HEAD : 2 * HEAD, :], proj[0:HEAD, cols], TN, preferred_element_type=F32
            )
            scores = jnp.where(live, scores * scale, MASKED)
            highest = jnp.max(scores, axis=0, keepdims=True)
            raised = jnp.exp(scores - highest)
            weights = (raised * (1.0 / jnp.sum(raised, axis=0, keepdims=True))).astype(BF16)
            got = jnp.dot(proj[2 * HEAD : 3 * HEAD, :], weights, preferred_element_type=F32)
            hbuf[pl.ds(pl.multiple_of(t * BLOCK + h * HEAD, 16), HEAD), cols] = got.astype(BF16)
            return carry

        lax.fori_loop(0, 2, columns, 0)

    for h in range(LOCAL_HEADS):
        attend(h)
        own_send(hbuf, h_send, h_recv, h, 0)
        own_send(hbuf, h_send, h_recv, h, 1)
        if h == 2:
            weights_step(4)
        if h >= 2:
            forward(hbuf, h_send, h_recv, h - 2)
    forward(hbuf, h_send, h_recv, 2)
    weights_step(5)
    forward(hbuf, h_send, h_recv, 3)
    near_wait(hbuf, h_send, h_recv)
    weights_step(6)
    far_wait(hbuf, h_send, h_recv)

    wout_copy.wait()
    got = jnp.dot(out_w[...], hbuf[...], preferred_element_type=F32)
    resid[...] = xbuf[pl.ds(pl.multiple_of(t * BLOCK, 16), BLOCK), :].astype(F32) + got + vt2[:, 3:4]

    def sums_of(i, acc):
        x = resid[pl.ds(pl.multiple_of(i * CHUNK, 16), CHUNK), :]
        return acc[0] + jnp.sum(x, axis=0, keepdims=True), acc[1] + jnp.sum(x * x, axis=0, keepdims=True)

    row_sum, row_squares = lax.fori_loop(0, BLOCK // CHUNK, sums_of, (zero_row, zero_row))
    stat[3] = jnp.concatenate([row_sum, row_squares, jnp.zeros((6, TILE), F32)], axis=0)
    targets = (right, left, across)
    for k in range(3):
        send(stat.at[3], stat.at[k], st_send, st_recv.at[k], (rank, targets[k]))
    weights_step(7)
    for k in range(3):
        arrived(stat.at[k], st_recv.at[k])
    sums = stat[0] + stat[1] + stat[2] + stat[3]
    row_mean = sums[0:1] * (1.0 / D)
    second = sums[1:2] * (1.0 / D)
    inv2 = lax.rsqrt(second - row_mean * row_mean + EPS)

    def encode(i, carry):
        rows = pl.ds(pl.multiple_of(i * CHUNK, 16), CHUNK)
        x = resid[rows, :]
        value = (x - row_mean) * inv2 * vt2[rows, 4:5] + vt2[rows, 5:6]
        proj[rows, :] = value.astype(BF16)
        return carry

    lax.fori_loop(0, BLOCK // CHUNK, encode, 0)
    pieces = []
    for j in range(4):
        chosen = (
            lax.broadcasted_iota(jnp.int32, (MROWS, TILE), 1)
            == 4 * lax.broadcasted_iota(jnp.int32, (MROWS, TILE), 0) + j
        )
        pick = jnp.where(chosen, 1.0, 0.0).astype(BF16)
        pieces.append(lax.dot_general(pick, proj[0:BLOCK, :], NT, preferred_element_type=F32))
    merged[...] = jnp.concatenate(pieces, axis=1).astype(BF16)

    same = pl.multiple_of(lax.rem(t, 2) * HALF, 16)
    other = pl.multiple_of(HALF - lax.rem(t, 2) * HALF, 16)
    upper = t // 2
    right_up, left_up = right // 2, left // 2
    right_rank = rank + (partner - rank) * right_up
    left_rank = rank + (partner - rank) * left_up

    def rs_copies(s):
        a_same, b_same = pl.ds(same, QUARTER), pl.ds(pl.multiple_of(same + QUARTER, 16), QUARTER)
        a_other, b_other = pl.ds(other, QUARTER), pl.ds(pl.multiple_of(other + QUARTER, 16), QUARTER)
        return (
            remote(pbuf.at[s, a_same], rel_a.at[s], rs_send.at[0], rs_recv.at[s, 0], (rank, right)),
            remote(pbuf.at[s, b_same], rel_b.at[s], rs_send.at[1], rs_recv.at[s, 1], (rank, left)),
            remote(pbuf.at[s, b_other], fb1.at[s], rs_send.at[2], rs_recv.at[s, 2], (right_rank, right)),
            remote(pbuf.at[s, a_other], fa1.at[s], rs_send.at[3], rs_recv.at[s, 3], (left_rank, left)),
            remote(rs_a.at[s], fa2.at[s], rs_send.at[4], rs_recv.at[s, 4], (right_rank, right)),
            remote(rs_b.at[s], fb2.at[s], rs_send.at[5], rs_recv.at[s, 5], (left_rank, left)),
            remote(pbuf.at[s, pl.ds(same, HALF)], xpb.at[s], rs_send.at[6], rs_recv.at[s, 6], (partner, t)),
        )

    def z_of(s):
        return (zwrap(z - s), zwrap(z + s)) if s else (z, zwrap(z - PHASES))

    def project(s):
        for k, zz in enumerate(z_of(s)):
            part = wbuf[zz].reshape(ZCOLS, D)
            got = lax.dot_general(merged[...], part, NT, preferred_element_type=F32)
            pbuf[s, :, k * ZCOLS : (k + 1) * ZCOLS] = got.astype(BF16)
        copies = rs_copies(s)
        for k in (0, 1, 6):
            copies[k].start()

    def direct(s):
        copies = rs_copies(s)
        for k in (2, 3):
            copies[k].start()

    def relay(s):
        copies = rs_copies(s)
        copies[0].wait_recv()
        own = pbuf[s, pl.ds(other, QUARTER), :].astype(F32)
        rs_a[s] = (rel_a[s].astype(F32) + own).astype(BF16)
        copies[4].start()
        copies[1].wait_recv()
        own = pbuf[s, pl.ds(pl.multiple_of(other + QUARTER, 16), QUARTER), :].astype(F32)
        rs_b[s] = (rel_b[s].astype(F32) + own).astype(BF16)
        copies[5].start()

    my_count = counts[2 * rank + upper]
    written = []

    def collect(s):
        copies = rs_copies(s)
        for k in (2, 3, 4, 5, 6):
            copies[k].wait_recv()
        local = pbuf[s, pl.ds(same, HALF), :].astype(F32)
        passed = xpb[s].astype(F32)
        is_upper = jnp.full((HALF, 2 * ZCOLS), upper, jnp.int32) > 0
        total = jnp.where(is_upper, passed, local)
        top = fa1[s].astype(F32) + fa2[s].astype(F32)
        bottom = fb1[s].astype(F32) + fb2[s].astype(F32)
        total = total + jnp.concatenate([top, bottom], axis=0)
        row = lax.broadcasted_iota(jnp.int32, (HALF, ZCOLS), 0) + lax.rem(t, 2) * HALF
        keep = 4 * row < my_count
        for k, zz in enumerate(z_of(s)):
            cols = pl.ds(pl.multiple_of(zz * ZCOLS, 128), ZCOLS)
            value = total[:, k * ZCOLS : (k + 1) * ZCOLS] + mbias[:, cols]
            obuf[:, cols] = jnp.where(keep, value, 0.0).astype(BF16)
            copy = pltpu.make_async_copy(obuf.at[:, cols], out.at[:, cols], out_sem.at[s, k])
            copy.start()
            written.append(copy)

    order = (1, 2, 3, 4, 5, 6, 7, 0)
    for n, s in enumerate(order):
        hand_wait(s)
        if s == 0:
            hand_wait(PHASES)
        project(s)
        if n in (1, 3, 5):
            weights_step(8 + n // 2)
        if n >= 2:
            relay(order[n - 2])
        if n >= 4:
            direct(order[n - 4])
    relay(order[6])
    direct(order[4])
    relay(order[7])
    for n in (5, 6, 7):
        direct(order[n])
    for s in order:
        collect(s)

    def all_left(ref, sem):
        remote(ref, ref, sem, part_recv, (partner, t)).wait_send()

    swap.wait_send()
    all_left(xbuf.at[pl.ds(0, 3 * BLOCK)], g_send)
    all_left(hbuf.at[pl.ds(0, 3 * BLOCK)], h_send)
    all_left(stat.at[pl.ds(0, 3)], st_send)
    all_left(wbuf.at[pl.ds(0, NY - 1), y, c, :, half_a], ya_send)
    all_left(wbuf.at[pl.ds(0, 3 * NZ // 4), :, c, :, half_b], yb_send)
    all_left(wbuf.at[pl.ds(0, NZ - 1), :, c, :, half_a], za_send)
    all_left(wbuf.at[pl.ds(0, NZ - 1), y, c, :, half_b], zb_send)
    all_left(wbuf.at[:, :, c], pf_send)
    for k in range(6):
        all_left(rel_a, rs_send.at[k])
    all_left(xpb, rs_send.at[6])
    for copy in written:
        copy.wait()


def per_device(
    patches,
    counts,
    first_gain,
    first_shift,
    in_weight,
    in_bias,
    out_weight,
    out_bias,
    second_gain,
    second_shift,
    merger_weight,
    merger_bias,
):
    any_spec = pl.BlockSpec(memory_space=pl.ANY)
    dma = pltpu.SemaphoreType.DMA
    return pl.pallas_call(
        kernel,
        out_shape=jax.ShapeDtypeStruct((HALF, LLMW), BF16),
        in_specs=[any_spec] * 12,
        out_specs=any_spec,
        scratch_shapes=[
            pltpu.VMEM((BLOCK, TILE), BF16),
            pltpu.VMEM((BLOCK, TILE), BF16),
            pltpu.VMEM((D, TILE), BF16),
            pltpu.VMEM((D, TILE), BF16),
            pltpu.VMEM((LOCAL_HEADS, 3, HEAD, D), BF16),
            pltpu.VMEM((BLOCK, D), BF16),
            pltpu.VMEM((8, D), F32),
            pltpu.VMEM((8, BLOCK), F32),
            pltpu.VMEM((3, BLOCK), F32),
            pltpu.VMEM((D, 8), F32),
            pltpu.VMEM((BLOCK, 8), F32),
            pltpu.VMEM((BLOCK, 8), F32),
            pltpu.VMEM((4, LLMW // 128, BLOCK), BF16),
            pltpu.VMEM((1, LLMW), F32),
            pltpu.VMEM((D, TILE), BF16),
            pltpu.VMEM((3 * BLOCK, TILE), BF16),
            pltpu.VMEM((4, 8, TILE), F32),
            pltpu.VMEM((BLOCK, TILE), F32),
            pltpu.VMEM((NZ, NY, 2, 32, D), BF16),
            pltpu.VMEM((MROWS, D), BF16),
            pltpu.VMEM((PHASES, MROWS, 2 * ZCOLS), BF16),
            pltpu.VMEM((PHASES, HALF, 2 * ZCOLS), BF16),
        ]
        + [pltpu.VMEM((PHASES, QUARTER, 2 * ZCOLS), BF16)] * 8
        + [pltpu.VMEM((HALF, LLMW), BF16)]
        + [pltpu.SMEM((256,), jnp.int32)]
        + [dma((16,)), dma((PHASES, 2)), dma, dma]
        + [dma, dma((2, 2, LOCAL_HEADS))] * 2
        + [dma, dma((3,))] * 2
        + [dma, dma((NZ, 3))]
        + [dma, dma((2, PHASES))] * 2
        + [dma, dma((NZ,)), dma((7,)), dma((PHASES, 7))],
        compiler_params=pltpu.CompilerParams(
            collective_id=0, has_side_effects=True, vmem_limit_bytes=60 * 1024 * 1024
        ),
        name="vision_block",
    )(
        counts,
        patches.T,
        jnp.transpose(in_weight, (1, 2, 0)).reshape(3, LOCAL_HEADS, HEAD, D),
        out_weight.T,
        first_gain,
        first_shift,
        in_bias,
        out_bias,
        second_gain,
        second_shift,
        jnp.transpose(merger_weight, (0, 2, 1)),
        merger_bias,
    )


def solution(mesh):
    return jax.shard_map(
        per_device,
        mesh=mesh,
        in_specs=(
            P("dp", "tensor"),
            P(),
            P(),
            P(),
            P(None, None, "tensor"),
            P(None, "tensor"),
            P(None, "tensor"),
            P("tensor"),
            P("tensor"),
            P("tensor"),
            P(None, "tensor", "dp"),
            P(),
        ),
        out_specs=P(("dp", "tensor"), None),
        check_vma=False,
    )
```

time: 121 us -> 81 us (0.67)
  the two profiles are of different devices: /device:TPU:18 before, /device:TPU:1 now
where the time goes in v2:
time: 81 us; the launch traced here: 80.9 us
  Pallas kernels  79 us (98%)
  local copies, waits for them, and re-layouts  1.87 us (2%)
    pallas_call x1, Pallas kernels, per_device(): pl.pallas_call(kernel, out_shape=jax.ShapeDtypeStruct((HALF, LLMW), BF16)...  79 us
    unnamed x1, local copies, waits for them, and re-layouts  1.87 us

profile of v2, /device:TPU:1, one launch (start us, length us, event | category | flops | bytes accessed | tf_op | source)
XLA Modules:
  0.0 80.9 jit_solution(5780632125281106347)
XLA Ops:
  0.0 79.0 %vision_block.1 = bf16[64,4096]{1,0:T(8,128)(2,1)} custom-call(s32[256]{0:T(256)} %counts_hbm.1, bf16[320,1024]{1,0:T(8,128)(2,1)} %bitcast.8, bf16[3,4,80,1280]{3,2,1,0:T(8,128)(2,1)} %bitcast.6, bf16[320,1280]{1,0:T(8,128)(2,1)} %bitcast.7, f32[1280]{0:T(1024)} %gain1.1, f32[1280]{0:T(1024)} %shift1.1, f32[3,320]{1,0:T(4,128)} %in_bias.1, f32[320]{0:T(512)} %out_bias.1, ...), custom_call_target="tpu_custom_call" | custom-call | tf_op jit(solution)/shard_map/vision_block/pallas_call | solution.py:554
  79.0 1.9 %copy.14 = bf16[64,4096]{1,0:T(8,128)(2,1)} copy(bf16[64,4096]{1,0:T(8,128)(2,1)} %vision_block.1) | data formatting | bytes 1048576

commit v3 on v2

--- a/solution.py
+++ b/solution.py
@@ -30,7 +30,7 @@
 F32 = jnp.float32
 BF16 = jnp.bfloat16
 CHUNK = 80
-SPLIT = 384
+SPLIT = 512
 
 NT = (((1,), (1,)), ((), ()))
 TN = (((0,), (0,)), ((), ()))
@@ -80,6 +80,7 @@
     fa2,
     fb1,
     fb2,
+    last,
     obuf,
     counts,
     local_sem,
@@ -104,6 +105,8 @@
     pf_recv,
     rs_send,
     rs_recv,
+    last_send,
+    last_recv,
 ):
     rank = lax.axis_index("dp")
     t = lax.axis_index("tensor")
@@ -124,7 +127,7 @@
     up = rank_of(zwrap(z + 1), y)
     down = rank_of(zwrap(z - 1), y)
 
-    peers = [(rank, right), (rank, left), (partner, right), (partner, left), (rank, across), (partner, t)]
+    peers = [(rank, right), (rank, left), (partner, right), (partner, left), (rank, across), (partner, across), (partner, t)]
     peers += [(rank_of(z, lax.rem(y + dy, NY)), t) for dy in range(1, NY)]
     peers += [(up, t), (down, t)]
     barrier = pltpu.get_barrier_semaphore()
@@ -145,6 +148,26 @@
     small += [load(shift2, vec2.at[5], 9), load(mbias_hbm, mbias.at[0], 10)]
     win_copies = [load(in_w_hbm.at[k], in_w.at[:, k], 11 + k) for k in range(3)]
     wout_copy = load(out_w_hbm, out_w, 14)
+    pl.semaphore_wait(barrier, len(peers))
+
+    def remote(src, dst, send, recv, device):
+        return pltpu.make_async_remote_copy(
+            src_ref=src, dst_ref=dst, send_sem=send, recv_sem=recv, device_id=device, device_id_type=MESH
+        )
+
+    def send(*args):
+        copy = remote(*args)
+        copy.start()
+
+    def piece(i):
+        return pl.ds(i * HEAD, HEAD)
+
+    swaps = [
+        remote(patches.at[piece(i), pl.ds(TILE, TILE)], slot1.at[piece(i)], part_send.at[i], part_recv.at[i], (partner, t))
+        for i in range(LOCAL_HEADS)
+    ]
+    for i in (0, 1, 2, 3):
+        swaps[i].start()
     mw_copy.wait()
     wbuf[z, y, c] = jnp.concatenate([mw[j] for j in range(4)], axis=1)
     for copy in small:
@@ -153,20 +176,6 @@
     vt2[...] = jnp.transpose(vec2[...])
     vt3[...] = jnp.transpose(jnp.concatenate([in_b[...], jnp.zeros((5, BLOCK), F32)], axis=0))
 
-    pl.semaphore_wait(barrier, len(peers))
-
-    def remote(src, dst, send, recv, device):
-        return pltpu.make_async_remote_copy(
-            src_ref=src, dst_ref=dst, send_sem=send, recv_sem=recv, device_id=device, device_id_type=MESH
-        )
-
-    def send(*args):
-        copy = remote(*args)
-        copy.start()
-
-    swap = remote(patches.at[:, pl.ds(TILE, TILE)], slot1, part_send, part_recv, (partner, t))
-    swap.start()
-
     def sub(buf, owner, h):
         return buf.at[pl.ds(pl.multiple_of(owner * BLOCK + h * HEAD, 16), HEAD)]
 
@@ -201,23 +210,20 @@
     half_a, half_b = pl.ds(0, SPLIT), pl.ds(SPLIT, D - SPLIT)
 
     def arrived(ref, recv):
-        remote(ref, ref, part_send, recv, (partner, t)).wait_recv()
-
-    def z_step(k):
-        for way, device in ((0, up), (1, down)):
-            if k > PHASES - way:
-                continue
-            zz = zwrap(z - (k - 1)) if way == 0 else zwrap(z + (k - 1))
-            ref = wbuf.at[zz, :, c, :, half_a]
-            send(ref, ref, za_send, za_recv.at[way, k - 1], (device, t))
-
-    def z_step_b(k):
-        for way, device in ((0, up), (1, down)):
-            if k > PHASES - way:
-                continue
-            zz = zwrap(z - (k - 1)) if way == 0 else zwrap(z + (k - 1))
-            ref = wbuf.at[zz, y, c, :, half_b]
-            send(ref, ref, zb_send, zb_recv.at[way, k - 1], (device, t))
+        remote(ref, ref, g_send, recv, (partner, t)).wait_recv()
+
+    def z_origin(way, k):
+        return zwrap(z - k) if way == 0 else zwrap(z + k)
+
+    def z_send_a(way, k):
+        if k <= PHASES - way:
+            ref = wbuf.at[z_origin(way, k - 1), :, c, :, half_a]
+            send(ref, ref, za_send, za_recv.at[way, k - 1], ((up, down)[way], t))
+
+    def z_send_b(way, k):
+        if k <= PHASES - way:
+            ref = wbuf.at[z_origin(way, k - 1), y, c, :, half_b]
+            send(ref, ref, zb_send, zb_recv.at[way, k - 1], ((up, down)[way], t))
 
     def blocks_of(k):
         if k == 0:
@@ -235,20 +241,13 @@
     def y_send_b(k):
         for index, zz in blocks_of(k):
             ref = y_block(zz, 0)
-            for dy in (1, 3):
+            for dy in (1, 3, 2):
                 send(ref, ref, yb_send, yb_recv.at[index, dy - 1], y_peer(dy))
-
-    def y_forward(k):
-        for turn, (index, zz) in enumerate(blocks_of(k)):
-            arrived(y_block(zz, 1), yb_recv.at[index, 0])
-            arrived(y_block(zz, 3), yb_recv.at[index, 2])
-            dy = 1 if turn == 0 else 3
-            ref = y_block(zz, dy)
-            send(ref, ref, yb_send, yb_recv.at[index, 1], y_peer(dy))
 
     def hand_over(k):
         for index, zz in blocks_of(k):
-            arrived(y_block(zz, 2), yb_recv.at[index, 1])
+            for dy in (1, 3, 2):
+                arrived(y_block(zz, dy), yb_recv.at[index, dy - 1])
             ref = wbuf.at[zz, :, c]
             send(ref, ref, pf_send, pf_recv.at[index], (partner, t))
 
@@ -260,47 +259,50 @@
         ref = wbuf.at[z, y, c, :, half_a]
         for dy in (1, 3, 2):
             send(ref, ref, ya_send, ya_recv.at[dy - 1], (rank_of(z, lax.rem(y + dy, NY)), t))
-        z_step_b(1)
+        z_send_b(0, 1)
+        z_send_b(1, 1)
         y_send_b(0)
 
     def weights_first():
         for dy in range(1, NY):
             arrived(wbuf.at[z, lax.rem(y + NY - dy, NY), c, :, half_a], ya_recv.at[dy - 1])
-        z_step(1)
+        z_send_a(0, 1)
+        z_send_a(1, 1)
 
     def weights_step(k):
+        if k == 0:
+            weights_first()
+            return
         if k <= PHASES:
             for way, (index, zz) in enumerate(blocks_of(k)):
+                arrived(wbuf.at[zz, :, c, :, half_a], za_recv.at[way, k - 1])
+                z_send_a(way, k + 1)
+            for way, (index, zz) in enumerate(blocks_of(k)):
                 arrived(wbuf.at[zz, y, c, :, half_b], zb_recv.at[way, k - 1])
-                arrived(wbuf.at[zz, :, c, :, half_a], za_recv.at[way, k - 1])
-            z_step(k + 1)
-            z_step_b(k + 1)
+                z_send_b(way, k + 1)
+        if k <= PHASES:
             y_send_b(k)
-        if k - 1 <= PHASES:
-            y_forward(k - 1)
-        if k >= 2:
-            hand_over(k - 2)
+        hand_over(k - 1)
 
     counted.wait()
     own0 = counts[2 * rank]
     other1 = counts[2 * partner + 1]
     tile_count = jnp.where(own0 > 0, own0, other1)
+    first.wait()
     weights_begin()
-    first.wait()
-    swap.wait_recv()
-
-    def choose(i, carry):
-        rows = pl.ds(pl.multiple_of(i * CHUNK, 16), CHUNK)
-        pick = jnp.full((CHUNK, TILE), own0, jnp.int32) > 0
-        value = jnp.where(pick, slot0[rows, :].astype(F32), slot1[rows, :].astype(F32))
-        xbuf[pl.ds(pl.multiple_of(t * BLOCK + i * CHUNK, 16), CHUNK), :] = value.astype(BF16)
-        return carry
-
-    lax.fori_loop(0, BLOCK // CHUNK, choose, 0)
+    own_live = jnp.full((HEAD, TILE), own0, jnp.int32) > 0
+
+    def choose(i):
+        swaps[i].wait_recv()
+        value = jnp.where(own_live, slot0[piece(i), :].astype(F32), slot1[piece(i), :].astype(F32))
+        xbuf[pl.ds(pl.multiple_of(t * BLOCK + i * HEAD, 16), HEAD), :] = value.astype(BF16)
+
+    for i in range(LOCAL_HEADS):
+        choose(i)
     for h in (0, 2, 1, 3):
         own_send(xbuf, g_send, g_recv, h, 0)
         own_send(xbuf, g_send, g_recv, (h + 1) if h % 2 == 0 else (h - 1), 1)
-    weights_first()
+    weights_step(0)
 
     def block_stats(owner):
         base = owner * BLOCK
@@ -343,7 +345,6 @@
         return carry
 
     lax.fori_loop(0, D // CHUNK, normalise, 0)
-    weights_step(3)
 
     for copy in win_copies:
         copy.wait()
@@ -374,15 +375,15 @@
         attend(h)
         own_send(hbuf, h_send, h_recv, h, 0)
         own_send(hbuf, h_send, h_recv, h, 1)
-        if h == 2:
-            weights_step(4)
+        if h == 1:
+            weights_step(3)
         if h >= 2:
             forward(hbuf, h_send, h_recv, h - 2)
+    weights_step(4)
     forward(hbuf, h_send, h_recv, 2)
-    weights_step(5)
     forward(hbuf, h_send, h_recv, 3)
     near_wait(hbuf, h_send, h_recv)
-    weights_step(6)
+    weights_step(5)
     far_wait(hbuf, h_send, h_recv)
 
     wout_copy.wait()
@@ -398,7 +399,7 @@
     targets = (right, left, across)
     for k in range(3):
         send(stat.at[3], stat.at[k], st_send, st_recv.at[k], (rank, targets[k]))
-    weights_step(7)
+    weights_step(6)
     for k in range(3):
         arrived(stat.at[k], st_recv.at[k])
     sums = stat[0] + stat[1] + stat[2] + stat[3]
@@ -430,6 +431,7 @@
     right_up, left_up = right // 2, left // 2
     right_rank = rank + (partner - rank) * right_up
     left_rank = rank + (partner - rank) * left_up
+    across_rank = rank + (partner - rank) * (across // 2)
 
     def rs_copies(s):
         a_same, b_same = pl.ds(same, QUARTER), pl.ds(pl.multiple_of(same + QUARTER, 16), QUARTER)
@@ -453,8 +455,16 @@
             got = lax.dot_general(merged[...], part, NT, preferred_element_type=F32)
             pbuf[s, :, k * ZCOLS : (k + 1) * ZCOLS] = got.astype(BF16)
         copies = rs_copies(s)
-        for k in (0, 1, 6):
+        for k in (0, 1, 6) if s else (6,):
             copies[k].start()
+
+    def last_copies():
+        mine_rows, their_rows = pl.ds(same, HALF), pl.ds(other, HALF)
+        return (
+            remote(pbuf.at[0, mine_rows], last.at[0], last_send, last_recv.at[0], (across_rank, across)),
+            remote(pbuf.at[0, their_rows], last.at[1], last_send, last_recv.at[1], (right_rank, right)),
+            remote(pbuf.at[0, their_rows], last.at[2], last_send, last_recv.at[2], (left_rank, left)),
+        )
 
     def direct(s):
         copies = rs_copies(s)
@@ -477,15 +487,21 @@
 
     def collect(s):
         copies = rs_copies(s)
-        for k in (2, 3, 4, 5, 6):
+        for k in (2, 3, 4, 5, 6) if s else (6,):
             copies[k].wait_recv()
+        if s == 0:
+            for copy in last_copies():
+                copy.wait_recv()
         local = pbuf[s, pl.ds(same, HALF), :].astype(F32)
         passed = xpb[s].astype(F32)
         is_upper = jnp.full((HALF, 2 * ZCOLS), upper, jnp.int32) > 0
         total = jnp.where(is_upper, passed, local)
-        top = fa1[s].astype(F32) + fa2[s].astype(F32)
-        bottom = fb1[s].astype(F32) + fb2[s].astype(F32)
-        total = total + jnp.concatenate([top, bottom], axis=0)
+        if s == 0:
+            total = total + last[0].astype(F32) + last[1].astype(F32) + last[2].astype(F32)
+        else:
+            top = fa1[s].astype(F32) + fa2[s].astype(F32)
+            bottom = fb1[s].astype(F32) + fb2[s].astype(F32)
+            total = total + jnp.concatenate([top, bottom], axis=0)
         row = lax.broadcasted_iota(jnp.int32, (HALF, ZCOLS), 0) + lax.rem(t, 2) * HALF
         keep = 4 * row < my_count
         for k, zz in enumerate(z_of(s)):
@@ -496,30 +512,41 @@
             copy.start()
             written.append(copy)
 
-    order = (1, 2, 3, 4, 5, 6, 7, 0)
-    for n, s in enumerate(order):
+    def phase(s):
         hand_wait(s)
         if s == 0:
             hand_wait(PHASES)
         project(s)
-        if n in (1, 3, 5):
-            weights_step(8 + n // 2)
-        if n >= 2:
-            relay(order[n - 2])
-        if n >= 4:
-            direct(order[n - 4])
-    relay(order[6])
-    direct(order[4])
-    relay(order[7])
-    for n in (5, 6, 7):
-        direct(order[n])
-    for s in order:
+
+    for s in (1, 2, 3, 4, 5):
+        phase(s)
+    weights_step(7)
+    for s in (1, 2, 3):
+        relay(s)
+        direct(s)
+    phase(6)
+    relay(4)
+    direct(4)
+    weights_step(8)
+    relay(5)
+    phase(7)
+    direct(5)
+    direct(6)
+    relay(6)
+    weights_step(9)
+    phase(0)
+    for copy in last_copies():
+        copy.start()
+    relay(7)
+    direct(7)
+    for s in (1, 2, 3, 4, 5, 6, 0, 7):
         collect(s)
 
     def all_left(ref, sem):
-        remote(ref, ref, sem, part_recv, (partner, t)).wait_send()
-
-    swap.wait_send()
+        remote(ref, ref, sem, part_recv.at[0], (partner, t)).wait_send()
+
+    for copy in swaps:
+        copy.wait_send()
     all_left(xbuf.at[pl.ds(0, 3 * BLOCK)], g_send)
     all_left(hbuf.at[pl.ds(0, 3 * BLOCK)], h_send)
     all_left(stat.at[pl.ds(0, 3)], st_send)
@@ -529,7 +556,8 @@
     all_left(wbuf.at[pl.ds(0, NZ - 1), y, c, :, half_b], zb_send)
     all_left(wbuf.at[:, :, c], pf_send)
     for k in range(6):
-        all_left(rel_a, rs_send.at[k])
+        all_left(rel_a.at[pl.ds(0, PHASES - 1)], rs_send.at[k])
+    all_left(last, last_send)
     all_left(xpb, rs_send.at[6])
     for copy in written:
         copy.wait()
@@ -581,14 +609,16 @@
             pltpu.VMEM((PHASES, HALF, 2 * ZCOLS), BF16),
         ]
         + [pltpu.VMEM((PHASES, QUARTER, 2 * ZCOLS), BF16)] * 8
+        + [pltpu.VMEM((3, HALF, 2 * ZCOLS), BF16)]
         + [pltpu.VMEM((HALF, LLMW), BF16)]
         + [pltpu.SMEM((256,), jnp.int32)]
-        + [dma((16,)), dma((PHASES, 2)), dma, dma]
+        + [dma((16,)), dma((PHASES, 2)), dma((LOCAL_HEADS,)), dma((LOCAL_HEADS,))]
         + [dma, dma((2, 2, LOCAL_HEADS))] * 2
-        + [dma, dma((3,))] * 2
+        + [dma, dma((3,))]
+        + [dma, dma((3,))]
         + [dma, dma((NZ, 3))]
         + [dma, dma((2, PHASES))] * 2
-        + [dma, dma((NZ,)), dma((7,)), dma((PHASES, 7))],
+        + [dma, dma((NZ,)), dma((7,)), dma((PHASES, 7)), dma, dma((3,))],
         compiler_params=pltpu.CompilerParams(
             collective_id=0, has_side_effects=True, vmem_limit_bytes=60 * 1024 * 1024
         ),

time: 81 us -> 79.5 us (0.981)
  Pallas kernels: 79 us -> 77.4 us
    pallas_call x1, Pallas kernels: 79 us -> 77.4 us  [per_device(): pl.pallas_call(kernel, out_shape=jax.ShapeDtypeStruct((HALF, LLMW), BF16)...]
where the time goes in v3:
time: 79.5 us; the launch traced here: 79.3 us
  Pallas kernels  77.4 us (97%)
  local copies, waits for them, and re-layouts  1.87 us (2%)
    pallas_call x1, Pallas kernels, per_device(): pl.pallas_call(kernel, out_shape=jax.ShapeDtypeStruct((HALF, LLMW), BF16)...  77.4 us
    unnamed x1, local copies, waits for them, and re-layouts  1.87 us

profile of v3, /device:TPU:1, one launch (start us, length us, event | category | flops | bytes accessed | tf_op | source)
XLA Modules:
  0.0 79.3 jit_solution(17986611239013707763)
XLA Ops:
  0.0 77.4 %vision_block.1 = bf16[64,4096]{1,0:T(8,128)(2,1)} custom-call(s32[256]{0:T(256)} %counts_hbm.1, bf16[320,1024]{1,0:T(8,128)(2,1)} %bitcast.8, bf16[3,4,80,1280]{3,2,1,0:T(8,128)(2,1)} %bitcast.6, bf16[320,1280]{1,0:T(8,128)(2,1)} %bitcast.7, f32[1280]{0:T(1024)} %gain1.1, f32[1280]{0:T(1024)} %shift1.1, f32[3,320]{1,0:T(4,128)} %in_bias.1, f32[320]{0:T(512)} %out_bias.1, ...), custom_call_target="tpu_custom_call" | custom-call | tf_op jit(solution)/shard_map/vision_block/pallas_call | solution.py:582
  77.5 1.9 %copy.14 = bf16[64,4096]{1,0:T(8,128)(2,1)} copy(bf16[64,4096]{1,0:T(8,128)(2,1)} %vision_block.1) | data formatting | bytes 1048576

commit v4 on v3

--- a/solution.py
+++ b/solution.py
@@ -449,22 +449,37 @@
     def z_of(s):
         return (zwrap(z - s), zwrap(z + s)) if s else (z, zwrap(z - PHASES))
 
+    def project_block(s, k):
+        part = wbuf[z_of(s)[k]].reshape(ZCOLS, D)
+        got = lax.dot_general(merged[...], part, NT, preferred_element_type=F32)
+        pbuf[s, :, k * ZCOLS : (k + 1) * ZCOLS] = got.astype(BF16)
+
     def project(s):
-        for k, zz in enumerate(z_of(s)):
-            part = wbuf[zz].reshape(ZCOLS, D)
-            got = lax.dot_general(merged[...], part, NT, preferred_element_type=F32)
-            pbuf[s, :, k * ZCOLS : (k + 1) * ZCOLS] = got.astype(BF16)
+        project_block(s, 0)
+        project_block(s, 1)
         copies = rs_copies(s)
-        for k in (0, 1, 6) if s else (6,):
+        for k in (0, 1, 6):
             copies[k].start()
 
-    def last_copies():
-        mine_rows, their_rows = pl.ds(same, HALF), pl.ds(other, HALF)
-        return (
-            remote(pbuf.at[0, mine_rows], last.at[0], last_send, last_recv.at[0], (across_rank, across)),
-            remote(pbuf.at[0, their_rows], last.at[1], last_send, last_recv.at[1], (right_rank, right)),
-            remote(pbuf.at[0, their_rows], last.at[2], last_send, last_recv.at[2], (left_rank, left)),
+    def straight(k):
+        mine_rows, their_rows, cols = pl.ds(same, HALF), pl.ds(other, HALF), pl.ds(k * ZCOLS, ZCOLS)
+        return tuple(
+            remote(pbuf.at[0, rows, cols], last.at[i, :, cols], last_send, last_recv.at[k, i], device)
+            for i, (rows, device) in enumerate(
+                (
+                    (mine_rows, (across_rank, across)),
+                    (their_rows, (right_rank, right)),
+                    (their_rows, (left_rank, left)),
+                    (mine_rows, (partner, t)),
+                )
+            )
         )
+
+    def straight_phase(k):
+        hand_wait(k * PHASES)
+        project_block(0, k)
+        for copy in straight(k):
+            copy.start()
 
     def direct(s):
         copies = rs_copies(s)
@@ -487,13 +502,14 @@
 
     def collect(s):
         copies = rs_copies(s)
-        for k in (2, 3, 4, 5, 6) if s else (6,):
-            copies[k].wait_recv()
-        if s == 0:
-            for copy in last_copies():
+        if s:
+            for k in (2, 3, 4, 5, 6):
+                copies[k].wait_recv()
+        else:
+            for copy in straight(0) + straight(1):
                 copy.wait_recv()
         local = pbuf[s, pl.ds(same, HALF), :].astype(F32)
-        passed = xpb[s].astype(F32)
+        passed = (xpb[s] if s else last[3]).astype(F32)
         is_upper = jnp.full((HALF, 2 * ZCOLS), upper, jnp.int32) > 0
         total = jnp.where(is_upper, passed, local)
         if s == 0:
@@ -514,13 +530,13 @@
 
     def phase(s):
         hand_wait(s)
-        if s == 0:
-            hand_wait(PHASES)
         project(s)
 
-    for s in (1, 2, 3, 4, 5):
+    for s in (1, 2, 3, 4):
         phase(s)
+    straight_phase(0)
     weights_step(7)
+    phase(5)
     for s in (1, 2, 3):
         relay(s)
         direct(s)
@@ -529,17 +545,19 @@
     direct(4)
     weights_step(8)
     relay(5)
+    direct(5)
     phase(7)
-    direct(5)
     direct(6)
+    for s in (1, 2, 3):
+        collect(s)
     relay(6)
+    direct(7)
+    collect(4)
     weights_step(9)
-    phase(0)
-    for copy in last_copies():
-        copy.start()
     relay(7)
-    direct(7)
-    for s in (1, 2, 3, 4, 5, 6, 0, 7):
+    collect(5)
+    straight_phase(1)
+    for s in (6, 7, 0):
         collect(s)
 
     def all_left(ref, sem):
@@ -557,8 +575,8 @@
     all_left(wbuf.at[:, :, c], pf_send)
     for k in range(6):
         all_left(rel_a.at[pl.ds(0, PHASES - 1)], rs_send.at[k])
-    all_left(last, last_send)
-    all_left(xpb, rs_send.at[6])
+    all_left(xpb.at[pl.ds(0, 4)], last_send)
+    all_left(xpb.at[pl.ds(0, PHASES - 1)], rs_send.at[6])
     for copy in written:
         copy.wait()
 
@@ -609,7 +627,7 @@
             pltpu.VMEM((PHASES, HALF, 2 * ZCOLS), BF16),
         ]
         + [pltpu.VMEM((PHASES, QUARTER, 2 * ZCOLS), BF16)] * 8
-        + [pltpu.VMEM((3, HALF, 2 * ZCOLS), BF16)]
+        + [pltpu.VMEM((4, HALF, 2 * ZCOLS), BF16)]
         + [pltpu.VMEM((HALF, LLMW), BF16)]
         + [pltpu.SMEM((256,), jnp.int32)]
         + [dma((16,)), dma((PHASES, 2)), dma((LOCAL_HEADS,)), dma((LOCAL_HEADS,))]
@@ -618,7 +636,7 @@
         + [dma, dma((3,))]
         + [dma, dma((NZ, 3))]
         + [dma, dma((2, PHASES))] * 2
-        + [dma, dma((NZ,)), dma((7,)), dma((PHASES, 7)), dma, dma((3,))],
+        + [dma, dma((NZ,)), dma((7,)), dma((PHASES, 7)), dma, dma((2, 4))],
         compiler_params=pltpu.CompilerParams(
             collective_id=0, has_side_effects=True, vmem_limit_bytes=60 * 1024 * 1024
         ),

time: 79.5 us -> 77.9 us (0.980)
  Pallas kernels: 77.4 us -> 75.9 us
    pallas_call x1, Pallas kernels: 77.4 us -> 75.9 us  [per_device(): pl.pallas_call(kernel, out_shape=jax.ShapeDtypeStruct((HALF, LLMW), BF16)...]
where the time goes in v4:
time: 77.9 us; the launch traced here: 77.8 us
  Pallas kernels  75.9 us (97%)
  local copies, waits for them, and re-layouts  1.87 us (2%)
    pallas_call x1, Pallas kernels, per_device(): pl.pallas_call(kernel, out_shape=jax.ShapeDtypeStruct((HALF, LLMW), BF16)...  75.9 us
    unnamed x1, local copies, waits for them, and re-layouts  1.87 us

profile of v4, /device:TPU:1, one launch (start us, length us, event | category | flops | bytes accessed | tf_op | source)
XLA Modules:
  0.0 77.8 jit_solution(14400195611418184390)
XLA Ops:
  0.0 75.9 %vision_block.1 = bf16[64,4096]{1,0:T(8,128)(2,1)} custom-call(s32[256]{0:T(256)} %counts_hbm.1, bf16[320,1024]{1,0:T(8,128)(2,1)} %bitcast.8, bf16[3,4,80,1280]{3,2,1,0:T(8,128)(2,1)} %bitcast.6, bf16[320,1280]{1,0:T(8,128)(2,1)} %bitcast.7, f32[1280]{0:T(1024)} %gain1.1, f32[1280]{0:T(1024)} %shift1.1, f32[3,320]{1,0:T(4,128)} %in_bias.1, f32[320]{0:T(512)} %out_bias.1, ...), custom_call_target="tpu_custom_call" | custom-call | tf_op jit(solution)/shard_map/vision_block/pallas_call | solution.py:600
  75.9 1.9 %copy.14 = bf16[64,4096]{1,0:T(8,128)(2,1)} copy(bf16[64,4096]{1,0:T(8,128)(2,1)} %vision_block.1) | data formatting | bytes 1048576

commit v5 on v4

--- a/solution.py
+++ b/solution.py
@@ -399,7 +399,6 @@
     targets = (right, left, across)
     for k in range(3):
         send(stat.at[3], stat.at[k], st_send, st_recv.at[k], (rank, targets[k]))
-    weights_step(6)
     for k in range(3):
         arrived(stat.at[k], st_recv.at[k])
     sums = stat[0] + stat[1] + stat[2] + stat[3]
@@ -532,8 +531,11 @@
         hand_wait(s)
         project(s)
 
-    for s in (1, 2, 3, 4):
-        phase(s)
+    phase(1)
+    phase(2)
+    weights_step(6)
+    phase(3)
+    phase(4)
     straight_phase(0)
     weights_step(7)
     phase(5)

time: 77.9 us -> 80.9 us (1.039)
  Pallas kernels: 75.9 us -> 78.9 us
    pallas_call x1, Pallas kernels: 75.9 us -> 78.9 us  [per_device(): pl.pallas_call(kernel, out_shape=jax.ShapeDtypeStruct((HALF, LLMW), BF16)...]
where the time goes in v5:
time: 80.9 us; the launch traced here: 80.8 us
  Pallas kernels  78.9 us (98%)
  local copies, waits for them, and re-layouts  1.87 us (2%)
    pallas_call x1, Pallas kernels, per_device(): pl.pallas_call(kernel, out_shape=jax.ShapeDtypeStruct((HALF, LLMW), BF16)...  78.9 us
    unnamed x1, local copies, waits for them, and re-layouts  1.87 us

profile of v5, /device:TPU:1, one launch (start us, length us, event | category | flops | bytes accessed | tf_op | source)
XLA Modules:
  0.0 80.8 jit_solution(12217263225548021647)
XLA Ops:
  0.0 78.9 %vision_block.1 = bf16[64,4096]{1,0:T(8,128)(2,1)} custom-call(s32[256]{0:T(256)} %counts_hbm.1, bf16[320,1024]{1,0:T(8,128)(2,1)} %bitcast.8, bf16[3,4,80,1280]{3,2,1,0:T(8,128)(2,1)} %bitcast.6, bf16[320,1280]{1,0:T(8,128)(2,1)} %bitcast.7, f32[1280]{0:T(1024)} %gain1.1, f32[1280]{0:T(1024)} %shift1.1, f32[3,320]{1,0:T(4,128)} %in_bias.1, f32[320]{0:T(512)} %out_bias.1, ...), custom_call_target="tpu_custom_call" | custom-call | tf_op jit(solution)/shard_map/vision_block/pallas_call | solution.py:602
  78.9 1.9 %copy.14 = bf16[64,4096]{1,0:T(8,128)(2,1)} copy(bf16[64,4096]{1,0:T(8,128)(2,1)} %vision_block.1) | data formatting | bytes 1048576
